TPU v7x, 256 devices: a whole 4x4x8 slice. The times are simulated.
256 devices in a mesh: rep: 2 (over y_lo), blk: 128 (over x, y_hi, z, core).
Axes of the slice: x: 4, y: 4 (y_hi: 2, y_lo: 2; y = y_hi * 2 + y_lo), z: 8, core: 2. Of those that a mesh axis runs over, the one named last changes fastest.
Arguments:
- a_blocks: float32 [128, 48, 256, 256], P('blk', 'rep'), may hold values from -0.375 to 0.375
- a_rows: int32 [128, 48], P('blk', 'rep'), may hold values from 0 to 255, as said below
- a_cols: int32 [128, 48], P('blk', 'rep'), may hold values from 0 to 255, as said below
- b_blocks: float32 [128, 6, 256, 256], P('blk'), may hold values from -6 to 6
- b_rows: int32 [128, 6], P('blk'), may hold values from 0 to 255, as said below
- b_cols: int32 [128, 6], P('blk'), may hold values from 0 to 255
- b_count: int32 [128], P('blk'), may hold values from 1 to 6, as said below
- c_rows: int32 [128, 16], P('blk'), may hold values from 0 to 255, as said below
- c_cols: int32 [128, 16], P('blk'), may hold values from 0 to 255
Outputs:
- iterate: float32 [128, 16, 256, 256], P('blk', 'rep')
Inputs may be any that keep to these rules, and one draw needn't show every extreme that they name: `a_rows`: entry [d, g] lies in the block rows d * 2 to d * 2 + 1. `a_cols`: entry [d, r * 6 * 4 + k * 4 + m] (m < 4) lies in the block rows e * 2 to e * 2 + 1 with e = (d + (r - 1) * 6 + k) modulo the size of blk. `b_rows`: entry [e, q] lies in the block rows e * 2 to e * 2 + 1. `b_count`: equals 6 on at least one index. `c_rows`: entry [d, t] lies in the block rows d * 2 to d * 2 + 1.
All inputs are finite; a program needn't handle non-finite values.
Results may differ from a plain program's by a relative error of at most 0.0003.
Values sent between devices are 32-bit elements; how exact they have to be, the bound alone decides.
No kernel may reach another device: no remote copies, remote signals or barrier semaphores. Data moves between devices by JAX's collectives and lax.ppermute only.
A program may use at most 128 MiB of HBM per device.

v0:
```python
import jax
import jax.numpy as jnp
from jax import lax
from jax.experimental import pallas as pl
from jax.experimental.pallas import tpu as pltpu
from jax.sharding import PartitionSpec as P


STEPS = 6
A_SLOTS = 4
PANEL = 6
HALF = 3
FRONT = 2
RUN = 8
REACH = 3
BOTH = ("rep", "blk")


def routed(value, target):
    n_rep, n_blk = lax.axis_size("rep"), lax.axis_size("blk")
    route = []
    for r in range(n_rep):
        for b in range(n_blk):
            r2, b2 = target(r, b)
            route.append((r * n_blk + b, r2 * n_blk + b2 % n_blk))
    return lax.ppermute(value, BOTH, route)


def upward(value):
    return routed(value, lambda r, b: (1 - r if (b // 2) % RUN == RUN - 1 else r, b + 2))


def downward(value):
    return routed(value, lambda r, b: (1 - r if (b // 2) % RUN == 0 else r, b - 2))


def other_replica(value):
    return routed(value, lambda r, b: (1 - r, b))


def other_core(value):
    return routed(value, lambda r, b: (r, b ^ 1))


def split(x):
    high = x.astype(jnp.bfloat16)
    low = (x - high.astype(jnp.float32)).astype(jnp.bfloat16)
    return high, low


def product(a, b):
    a_high, a_low = split(a)
    b_high, b_low = split(b)

    def dot(x, y):
        return jnp.dot(x, y, preferred_element_type=jnp.float32)

    return dot(a_high, b_high) + (dot(a_high, b_low) + dot(a_low, b_high))


def multiply_kernel(
    n_whole, n_split, first, last, info, a_rows, a_cols, c_rows, c_cols, *refs
):
    n_panels = n_whole + n_split
    notes, a_hbm, refs = refs[:n_panels], refs[n_panels], refs[n_panels + 1 :]
    whole, refs = refs[:n_whole], refs[n_whole:]
    pieces, refs = refs[: 4 * n_split], refs[4 * n_split :]
    if not first:
        acc_in, refs = refs[0], refs[1:]
    if last:
        keep_out, send_out, refs = refs[0], refs[1], refs[2:]
    else:
        acc_out, refs = refs[0], refs[1:]
    acc, a_buf, b_buf, work, hits, count, sems, acc_sem = refs
    size = a_buf.shape[-1]
    n_targets = acc.shape[0]
    half = n_targets // 2

    if not first:
        load = pltpu.make_async_copy(acc_in, acc, acc_sem.at[0])
        load.start()

    per_panel = A_SLOTS * PANEL
    count[0] = 0

    for p in range(n_panels):
        group = info[p]

        @pl.when(group >= 0)
        def _():
            @pl.loop(0, notes[p][2 * PANEL])
            def _(q):
                @pl.loop(0, A_SLOTS)
                def _(m):
                    slot = group * A_SLOTS + m

                    @pl.when(a_cols[slot] == notes[p][q])
                    def _():
                        row, col = a_rows[slot], notes[p][PANEL + q]
                        mask = jnp.int32(0)
                        for t in range(n_targets):
                            hit = (c_rows[t] == row) & (c_cols[t] == col)
                            mask = mask + jnp.where(hit, 1 << t, 0)

                        @pl.when(mask != 0)
                        def _():
                            n = count[0]
                            work[n] = p * per_panel + m * PANEL + q
                            hits[n] = mask
                            count[0] = n + 1

    total = count[0]

    def fetch_b(source, buf):
        pltpu.make_async_copy(source, b_buf.at[buf], sems.at[1, buf]).start()

    def fetch(n, buf):
        i = work[n]
        panel = lax.div(i, per_panel)
        rest = lax.rem(i, per_panel)
        a_slot = info[panel] * A_SLOTS + lax.div(rest, PANEL)
        q = lax.rem(rest, PANEL)
        pltpu.make_async_copy(a_hbm.at[a_slot], a_buf.at[buf], sems.at[0, buf]).start()
        for p in range(n_whole):

            @pl.when(panel == p)
            def _():
                fetch_b(whole[p].at[q], buf)

        second = (lax.rem(q, 2) != info[n_panels + panel]).astype(jnp.int32)
        place = lax.div(q, 2)
        tail = (place == FRONT).astype(jnp.int32)
        which = (panel - n_whole) * 4 + tail * 2 + second
        row = pl.multiple_of((place - tail * FRONT) * size, size)
        for p in range(4 * n_split):

            @pl.when(which == p)
            def _():
                if p % 4 < 2:
                    fetch_b(pieces[p].at[pl.ds(row, size), :], buf)
                else:
                    fetch_b(pieces[p].at[pl.ds((p % 4 - 2) * size if pieces[p].shape[0] > size else 0, size), :], buf)

    @pl.when(total > 0)
    def _():
        fetch(0, 0)

    if first:
        acc[...] = jnp.zeros_like(acc)
    else:
        load.wait()

    @pl.loop(0, total)
    def _(n):
        buf = lax.rem(n, 2)

        @pl.when(n + 1 < total)
        def _():
            fetch(n + 1, 1 - buf)

        pltpu.make_async_copy(a_hbm.at[0], a_buf.at[buf], sems.at[0, buf]).wait()
        pltpu.make_async_copy(a_hbm.at[0], b_buf.at[buf], sems.at[1, buf]).wait()
        term = product(a_buf[buf], b_buf[buf])
        mask = hits[n]

        @pl.loop(0, n_targets)
        def _(t):
            @pl.when(lax.rem(lax.shift_right_logical(mask, t), 2) == 1)
            def _():
                acc[t] = acc[t] + term

    if last:
        out = pltpu.make_async_copy(acc.at[pl.ds(half, half)], send_out, acc_sem.at[0])
        out.start()
        kept = pltpu.make_async_copy(acc.at[pl.ds(0, half)], keep_out, acc_sem.at[1])
        kept.start()
        out.wait()
        kept.wait()
    else:
        out = pltpu.make_async_copy(acc, acc_out, acc_sem.at[0])
        out.start()
        out.wait()


def multiply(info, tables, notes, a_blocks, whole, pieces, acc, last, n_targets):
    n_whole, n_split = len(whole), len(pieces) // 4
    n_panels = n_whole + n_split
    size = a_blocks.shape[-1]
    first = acc is None
    smem = pl.BlockSpec(memory_space=pltpu.SMEM)
    anywhere = pl.BlockSpec(memory_space=pl.ANY)
    stays = pl.BlockSpec(memory_space=pltpu.HBM)
    full = jax.ShapeDtypeStruct((n_targets, size, size), jnp.float32)
    part = jax.ShapeDtypeStruct((n_targets // 2, size, size), jnp.float32)
    numbers = [info, *tables, *notes]
    operands = [*numbers, a_blocks, *whole, *pieces] + ([] if first else [acc])

    def kernel(*refs):
        multiply_kernel(n_whole, n_split, first, last, *refs)

    return pl.pallas_call(
        kernel,
        out_shape=[part, part] if last else full,
        in_specs=[smem] * len(numbers) + [stays] + [anywhere] * (len(operands) - len(numbers) - 1),
        out_specs=[anywhere, anywhere] if last else anywhere,
        scratch_shapes=[
            pltpu.VMEM((n_targets, size, size), jnp.float32),
            pltpu.VMEM((2, size, size), jnp.float32),
            pltpu.VMEM((2, size, size), jnp.float32),
            pltpu.SMEM((n_panels * A_SLOTS * PANEL,), jnp.int32),
            pltpu.SMEM((n_panels * A_SLOTS * PANEL,), jnp.int32),
            pltpu.SMEM((1,), jnp.int32),
            pltpu.SemaphoreType.DMA((2, 2)),
            pltpu.SemaphoreType.DMA((2,)),
        ],
        cost_estimate=pl.CostEstimate(
            flops=2 * 8 * size**3, bytes_accessed=12 * 2**20, transcendentals=0
        ),
        compiler_params=pltpu.CompilerParams(vmem_limit_bytes=8 * 2**20),
        name="multiply",
    )(*operands)


def local(a_blocks, a_rows, a_cols, b_blocks, b_rows, b_cols, b_count, c_rows, c_cols):
    replica = lax.axis_index("rep")
    index = lax.axis_index("blk")
    core = index % 2
    z = (index // 2) % RUN
    lower = replica == 0
    a_blocks = a_blocks[0]
    b_blocks = b_blocks[0]
    size = a_blocks.shape[-1]
    n_targets = c_rows.shape[1]
    half = n_targets // 2

    numbers = jnp.concatenate([b_rows[0], b_cols[0], b_count, jnp.zeros((3,), jnp.int32)])
    notes = jnp.pad(numbers.astype(jnp.float32)[None], ((0, 7), (0, size - numbers.shape[0])))
    mine = lax.dynamic_index_in_dim(
        b_blocks.reshape(HALF, 2, size, size), replica, 1, keepdims=False
    )
    front = jnp.concatenate([mine[:FRONT].reshape(FRONT * size, size), notes], 0)
    up = down = front
    up_tail = down_tail = mine[FRONT]

    def own_first(x):
        return jnp.where(lower, x, jnp.roll(x, half))

    target_rows = own_first(c_rows[0])
    target_cols = own_first(c_cols[0])
    tables = [a_rows[0], a_cols[0], target_rows, target_cols]

    def group_of(distance):
        group = distance + jnp.where(lower, STEPS, 0)
        return jnp.where((group >= 0) & (group < STEPS), group, -1)

    def noted(piece):
        return piece[FRONT * size, : numbers.shape[0]].astype(jnp.int32)

    side = jnp.where(lower, -1, 1)
    zero = jnp.int32(0)

    def run(stages, whole, acc, last):
        pieces, notes, groups, lows = [], [], [], []
        for p, m, g, l in stages:
            pieces += p
            notes += m
            groups += g
            lows += l
        info = jnp.stack(groups + lows).astype(jnp.int32)
        return multiply(info, tables, notes, a_blocks, whole, pieces, acc, last, n_targets)

    ups, downs, up_tails, down_tails = [], [], [], []
    for _ in range(1, REACH + 1):
        up, down = upward(up), downward(down)
        up_tail, down_tail = upward(up_tail), downward(down_tail)
        ups.append(up)
        downs.append(down)
        up_tails.append(up_tail)
        down_tails.append(down_tail)
    partner = other_core(b_blocks)
    notes = [numbers, other_core(numbers)]
    stages = [([], notes, [group_of(zero), group_of(1 - 2 * core)], [zero, zero])]
    for s in range(1, REACH + 1):
        up, down, up_tail, down_tail = ups[s - 1], downs[s - 1], up_tails[s - 1], down_tails[s - 1]
        kept, given = jnp.where(lower, up, down), jnp.where(lower, down, up)
        rest = other_replica(given)
        kept_tail = jnp.where(lower, up_tail, down_tail)
        rest_tail = other_replica(jnp.where(lower, down_tail, up_tail))
        kept2, rest2 = other_core(kept), other_core(rest)
        tails = jnp.concatenate([kept_tail, rest_tail], 0)
        tails2 = other_core(tails)
        crossed = jnp.where(lower, z < s, z + s > RUN - 1).astype(jnp.int32)
        low = lax.bitwise_xor(replica, crossed)
        notes = [noted(kept), noted(kept2)]
        groups = [group_of(2 * s * side), group_of(2 * s * side + 1 - 2 * core)]
        pieces = [kept, rest, tails, tails, kept2, rest2, tails2, tails2]
        stages.append((pieces, notes, groups, [low, low]))
    acc = run(stages[:REACH], [b_blocks, partner], None, False)
    keep, send = run(stages[REACH:], [], acc, True)
    summed = keep + other_replica(send)
    diagonal = (target_rows[:half] == target_cols[:half]).astype(jnp.float32)
    identity = jnp.eye(size, dtype=jnp.float32)
    result = 1.5 * diagonal[:, None, None] * identity[None, :, :] - 0.5 * summed
    return result[None]


def solution(mesh):
    return jax.shard_map(
        local,
        mesh=mesh,
        in_specs=(
            P("blk", "rep", None, None),
            P("blk", "rep"),
            P("blk", "rep"),
            P("blk", None, None, None),
            P("blk", None),
            P("blk", None),
            P("blk"),
            P("blk", None),
            P("blk", None),
        ),
        out_specs=P("blk", "rep", None, None),
        check_vma=False,
    )
```

profile of v0, /device:TPU:8, one launch (start us, length us, event | category | flops | bytes accessed | tf_op | source)
XLA Modules:
  0.0 175.4 jit_solution(16311390972791227952)
XLA Ops:
  0.0 1.0 dynamic-slice_bitcast_fusion
  1.0 9.1 %collective-permute-start.11 = (f32[256,256]{1,0:T(8,128)S(1)}, f32[256,256]{1,0:T(8,128)}, u32[]{:S(2)}, u32[]{:S(2)}) collective-permute-start(f32[256,256]{1,0:T(8,128)S(1)} %dynamic-slice_bitcast_fusion), channel_id=1, source_target_pairs={{0,254},{1,255},{2,0},{3,1},{4,2},{5,3},{6,4},{7,5},{8,6},{9,7},{1... | collective-permute-start | bytes 786440 | tf_op jit(solution)/shard_map/ppermute | solution.py:26
  10.2 1.2 constant_dynamic-slice_fusion
  12.1 0.8 fusion.2
  12.8 0.8 select_maximum_fusion
  13.7 6.2 %collective-permute-start.3 = (f32[520,256]{1,0:T(8,128)}, f32[520,256]{1,0:T(8,128)S(1)}, u32[]{:S(2)}, u32[]{:S(2)}) collective-permute-start(f32[520,256]{1,0:T(8,128)} %select_maximum_fusion), channel_id=1, source_target_pairs={{0,254},{1,255},{2,0},{3,1},{4,2},{5,3},{6,4},{7,5},{8,6},{9,7},{1... | collective-permute-start | bytes 1597448 | tf_op jit(solution)/shard_map/ppermute | solution.py:26
  19.9 0.1 slice_bitcast_fusion.1
  20.0 0.1 slice_bitcast_fusion.3
  20.1 0.1 pad_add_fusion.refs_5_
  20.1 0.1 broadcast_select_fusion.12
  20.2 2.3 %collective-permute-start.12 = (f32[256,256]{1,0:T(8,128)}, f32[256,256]{1,0:T(8,128)}, u32[]{:S(2)}, u32[]{:S(2)}) collective-permute-start(f32[256,256]{1,0:T(8,128)} %collective-permute-done.11), channel_id=1, source_target_pairs={{0,254},{1,255},{2,0},{3,1},{4,2},{5,3},{6,4},{7,5},{8,6},{9,7},{1... | collective-permute-start | bytes 786440 | tf_op jit(solution)/shard_map/ppermute | solution.py:26
  22.5 1.1 collective-permute-done.8
  23.7 1.8 %broadcast_select_fusion.9 = (f32[256,256]{1,0:T(8,128)S(1)}, f32[256,256]{1,0:T(8,128)}) fusion(f32[256,256]{1,0:T(8,128)} %collective-permute-done.8, f32[256,256]{1,0:T(8,128)} %collective-permute-done.11, pred[]{:T(512)S(6)} %eq.16), kind=kLoop, calls=%fused_computation.18 | loop fusion | flops 131072 | bytes 1048577 | tf_op jit(solution)/shard_map/jit(_where)/select_n | solution.py:287
  25.4 3.1 %collective-permute-start.22 = (f32[256,256]{1,0:T(8,128)}, f32[256,256]{1,0:T(8,128)}, u32[]{:S(2)}, u32[]{:S(2)}) collective-permute-start(f32[256,256]{1,0:T(8,128)} %get-tuple-element.18), channel_id=1, source_target_pairs={{0,128},{1,129},{2,130},{3,131},{4,132},{5,133},{6,134},{7,135},{8... | collective-permute-start | bytes 786440 | tf_op jit(solution)/shard_map/ppermute | solution.py:26
  28.5 0.1 pad_add_fusion.1.refs_0_
  28.6 0.1 stack.54.refs_0_
  28.7 7.9 %collective-permute-done.12 = f32[256,256]{1,0:T(8,128)} collective-permute-done((f32[256,256]{1,0:T(8,128)}, f32[256,256]{1,0:T(8,128)}, u32[]{:S(2)}, u32[]{:S(2)}) %collective-permute-start.12) | collective-permute-done | bytes 262176 | tf_op jit(solution)/shard_map/ppermute | solution.py:26
  36.6 2.7 %collective-permute-done.9 = f32[256,256]{1,0:T(8,128)} collective-permute-done((f32[256,256]{1,0:T(8,128)}, f32[256,256]{1,0:T(8,128)}, u32[]{:S(2)}, u32[]{:S(2)}) %collective-permute-start.9) | collective-permute-done | bytes 262176 | tf_op jit(solution)/shard_map/ppermute | solution.py:26
  39.3 1.1 broadcast_select_fusion.7
  40.4 0.1 collective-permute-start.20
  40.5 0.1 collective-permute-start.1
  40.6 6.3 %collective-permute-start.4 = (f32[520,256]{1,0:T(8,128)S(1)}, f32[520,256]{1,0:T(8,128)S(1)}, u32[]{:S(2)}, u32[]{:S(2)}) collective-permute-start(f32[520,256]{1,0:T(8,128)S(1)} %collective-permute-done.3), channel_id=1, source_target_pairs={{0,254},{1,255},{2,0},{3,1},{4,2},{5,3},{6,4},{7,5},{8,6},{9,7},{1... | collective-permute-start | bytes 1597448 | tf_op jit(solution)/shard_map/ppermute | solution.py:26
  46.9 1.0 pad_maximum_fusion.1.refs_16_.refs_17_
  47.9 4.4 %collective-permute-start.26 = (f32[256,256]{1,0:T(8,128)S(1)}, f32[256,256]{1,0:T(8,128)S(1)}, u32[]{:S(2)}, u32[]{:S(2)}) collective-permute-start(f32[256,256]{1,0:T(8,128)S(1)} %get-tuple-element.16), channel_id=1, source_target_pairs={{0,128},{1,129},{2,130},{3,131},{4,132},{5,133},{6,134},{7,135},{8... | collective-permute-start | bytes 786440 | tf_op jit(solution)/shard_map/ppermute | solution.py:26
  52.3 0.6 collective-permute-done.10
  52.9 0.7 collective-permute-start.13
  53.6 0.1 broadcast_select_fusion.1
  53.7 10.8 %collective-permute-done.13 = f32[256,256]{1,0:T(8,128)S(1)} collective-permute-done((f32[256,256]{1,0:T(8,128)}, f32[256,256]{1,0:T(8,128)S(1)}, u32[]{:S(2)}, u32[]{:S(2)}) %collective-permute-start.13) | collective-permute-done | bytes 262176 | tf_op jit(solution)/shard_map/ppermute | solution.py:26
  64.6 4.4 %collective-permute-start.14 = (f32[256,256]{1,0:T(8,128)S(1)}, f32[256,256]{1,0:T(8,128)S(1)}, u32[]{:S(2)}, u32[]{:S(2)}) collective-permute-start(f32[256,256]{1,0:T(8,128)S(1)} %get-tuple-element.20), channel_id=1, source_target_pairs={{0,128},{1,129},{2,130},{3,131},{4,132},{5,133},{6,134},{7,135},{8... | collective-permute-start | bytes 786440 | tf_op jit(solution)/shard_map/ppermute | solution.py:26
  69.0 7.3 %collective-permute-start.5 = (f32[520,256]{1,0:T(8,128)S(1)}, f32[520,256]{1,0:T(8,128)S(1)}, u32[]{:S(2)}, u32[]{:S(2)}) collective-permute-start(f32[520,256]{1,0:T(8,128)S(1)} %collective-permute-done.4), channel_id=1, source_target_pairs={{0,254},{1,255},{2,0},{3,1},{4,2},{5,3},{6,4},{7,5},{8,6},{9,7},{1... | collective-permute-start | bytes 1597448 | tf_op jit(solution)/shard_map/ppermute | solution.py:26
  76.3 0.1 collective-permute-start.18
  76.5 1.3 collective-permute-start.21
  77.7 0.1 broadcast_select_fusion
  77.8 10.9 %collective-permute-done.2 = f32[520,256]{1,0:T(8,128)S(1)} collective-permute-done((f32[520,256]{1,0:T(8,128)S(1)}, f32[520,256]{1,0:T(8,128)S(1)}, u32[]{:S(2)}, u32[]{:S(2)}) %collective-permute-start.2) | collective-permute-done | bytes 532512 | tf_op jit(solution)/shard_map/ppermute | solution.py:26
  88.7 1.2 collective-permute-start.25
  90.0 0.3 collective-permute-start.19
  90.3 0.7 collective-permute-done.21.refs_15_
  90.9 0.9 collective-permute-start.7
  91.9 0.1 collective-permute-start.23
  92.0 0.5 collective-permute-start.6
  92.5 11.2 %collective-permute-done.25.refs_23_ = f32[520,256]{1,0:T(8,128)S(1)} collective-permute-done((f32[520,256]{1,0:T(8,128)S(1)}, f32[520,256]{1,0:T(8,128)S(1)}, u32[]{:S(2)}, u32[]{:S(2)}) %collective-permute-start.25) | collective-permute-done | bytes 532512 | tf_op jit(solution)/shard_map/ppermute | solution.py:26
  103.7 0.5 collective-permute-start.16
  104.2 10.4 %collective-permute-done.7.refs_9_ = f32[520,256]{1,0:T(8,128)S(1)} collective-permute-done((f32[520,256]{1,0:T(8,128)S(1)}, f32[520,256]{1,0:T(8,128)S(1)}, u32[]{:S(2)}, u32[]{:S(2)}) %collective-permute-start.7) | collective-permute-done | bytes 532512 | tf_op jit(solution)/shard_map/ppermute | solution.py:26
  114.7 7.0 %multiply.2.refs_16_ = f32[16,256,256]{2,1,0:T(8,128)S(1)} custom-call(s32[12]{0:T(128)S(1)} %stack.54.refs_0_, s32[24]{0:T(128)S(1)} %bitcast.63, s32[24]{0:T(128)S(1)} %bitcast.65, s32[16]{0:T(128)S(1)} %get-tuple-element.26.refs_3_, s32[16]{0:T(128)S(1)} %get-tuple-element.25.refs_4_, s32[16]{0:T(128)S(1)} %pad_add_fusion.refs_5_, ...), custom_call_target="tpu_custom_call" | custom-call | flops 268435456 | bytes 12582912 | tf_op jit(solution)/shard_map/multiply/pallas_call | solution.py:201
  121.7 1.2 multiply.3
  123.0 6.0 %collective-permute-start.29 = (f32[8,256,256]{2,1,0:T(8,128)S(1)}, f32[8,256,256]{2,1,0:T(8,128)S(1)}, u32[]{:S(2)}, u32[]{:S(2)}) collective-permute-start(f32[8,256,256]{2,1,0:T(8,128)S(1)} %get-tuple-element.8), channel_id=1, source_target_pairs={{0,128},{1,129},{2,130},{3,131},{4,132},{5,133},{6,134},{7,135},{8... | collective-permute-start | bytes 6291464 | tf_op jit(solution)/shard_map/ppermute | solution.py:26
  129.1 44.7 %collective-permute-done.29 = f32[8,256,256]{2,1,0:T(8,128)S(1)} collective-permute-done((f32[8,256,256]{2,1,0:T(8,128)S(1)}, f32[8,256,256]{2,1,0:T(8,128)S(1)}, u32[]{:S(2)}, u32[]{:S(2)}) %collective-permute-start.29) | collective-permute-done | bytes 2097184 | tf_op jit(solution)/shard_map/ppermute | solution.py:26
  173.7 1.7 subtract_bitcast_fusion
  (63 shorter events, 0.4 us)
Async XLA Ops:
  0.0 20.1 %copy-start.6 = (s32[1,6]{1,0:T(1,128)S(1)}, s32[1,6]{1,0:T(1,128)}, u32[]{:S(2)}) copy-start(s32[1,6]{1,0:T(1,128)} %param.13) | copy-start | bytes 76
  0.0 20.1 %copy-start.5 = (s32[1,6]{1,0:T(1,128)S(1)}, s32[1,6]{1,0:T(1,128)}, u32[]{:S(2)}) copy-start(s32[1,6]{1,0:T(1,128)} %param.14) | copy-start | bytes 76
  0.0 19.9 %copy-start.3 = (s32[1,16]{1,0:T(1,128)S(1)}, s32[1,16]{1,0:T(1,128)}, u32[]{:S(2)}) copy-start(s32[1,16]{1,0:T(1,128)} %param.17) | copy-start | bytes 196
  0.0 20.0 %copy-start.4 = (s32[1,16]{1,0:T(1,128)S(1)}, s32[1,16]{1,0:T(1,128)}, u32[]{:S(2)}) copy-start(s32[1,16]{1,0:T(1,128)} %param.16) | copy-start | bytes 196
  1.0 19.2 %collective-permute-start.11 = (f32[256,256]{1,0:T(8,128)S(1)}, f32[256,256]{1,0:T(8,128)}, u32[]{:S(2)}, u32[]{:S(2)}) collective-permute-start(f32[256,256]{1,0:T(8,128)S(1)} %dynamic-slice_bitcast_fusion), channel_id=1, source_target_pairs={{0,254},{1,255},{2,0},{3,1},{4,2},{5,3},{6,4},{7,5},{8,6},{9,7},{1... | collective-permute-start | bytes 786440 | tf_op jit(solution)/shard_map/ppermute | solution.py:26
  10.2 13.5 %collective-permute-start.8 = (f32[256,256]{1,0:T(8,128)S(1)}, f32[256,256]{1,0:T(8,128)}, u32[]{:S(2)}, u32[]{:S(2)}) collective-permute-start(f32[256,256]{1,0:T(8,128)S(1)} %dynamic-slice_bitcast_fusion), channel_id=1, source_target_pairs={{0,2},{1,3},{2,4},{3,5},{4,6},{5,7},{6,8},{7,9},{8,10},{9,11},{10,... | collective-permute-start | bytes 786440 | tf_op jit(solution)/shard_map/ppermute | solution.py:26
  10.2 104.5 %slice-start = ((s8[6291456]{0:T(1024)(128)(4,1)}), s8[2097152]{0:T(1024)(128)(4,1)S(1)}, s32[]{:S(2)}) async-start(s8[6291456]{0:T(1024)(128)(4,1)} %bitcast.55), calls=%async_computation | async-start | bytes 4194304
  13.7 26.8 %collective-permute-start = (f32[520,256]{1,0:T(8,128)}, f32[520,256]{1,0:T(8,128)S(1)}, u32[]{:S(2)}, u32[]{:S(2)}) collective-permute-start(f32[520,256]{1,0:T(8,128)} %select_maximum_fusion), channel_id=1, source_target_pairs={{0,2},{1,3},{2,4},{3,5},{4,6},{5,7},{6,8},{7,9},{8,10},{9,11},{10,... | collective-permute-start | bytes 1597448 | tf_op jit(solution)/shard_map/ppermute | solution.py:26
  13.7 26.9 %collective-permute-start.3 = (f32[520,256]{1,0:T(8,128)}, f32[520,256]{1,0:T(8,128)S(1)}, u32[]{:S(2)}, u32[]{:S(2)}) collective-permute-start(f32[520,256]{1,0:T(8,128)} %select_maximum_fusion), channel_id=1, source_target_pairs={{0,254},{1,255},{2,0},{3,1},{4,2},{5,3},{6,4},{7,5},{8,6},{9,7},{1... | collective-permute-start | bytes 1597448 | tf_op jit(solution)/shard_map/ppermute | solution.py:26
  20.2 16.4 %collective-permute-start.12 = (f32[256,256]{1,0:T(8,128)}, f32[256,256]{1,0:T(8,128)}, u32[]{:S(2)}, u32[]{:S(2)}) collective-permute-start(f32[256,256]{1,0:T(8,128)} %collective-permute-done.11), channel_id=1, source_target_pairs={{0,254},{1,255},{2,0},{3,1},{4,2},{5,3},{6,4},{7,5},{8,6},{9,7},{1... | collective-permute-start | bytes 786440 | tf_op jit(solution)/shard_map/ppermute | solution.py:26
  23.7 15.6 %collective-permute-start.9 = (f32[256,256]{1,0:T(8,128)}, f32[256,256]{1,0:T(8,128)}, u32[]{:S(2)}, u32[]{:S(2)}) collective-permute-start(f32[256,256]{1,0:T(8,128)} %collective-permute-done.8), channel_id=1, source_target_pairs={{0,2},{1,3},{2,4},{3,5},{4,6},{5,7},{6,8},{7,9},{8,10},{9,11},{10,... | collective-permute-start | bytes 786440 | tf_op jit(solution)/shard_map/ppermute | solution.py:26
  25.4 14.9 %collective-permute-start.22 = (f32[256,256]{1,0:T(8,128)}, f32[256,256]{1,0:T(8,128)}, u32[]{:S(2)}, u32[]{:S(2)}) collective-permute-start(f32[256,256]{1,0:T(8,128)} %get-tuple-element.18), channel_id=1, source_target_pairs={{0,128},{1,129},{2,130},{3,131},{4,132},{5,133},{6,134},{7,135},{8... | collective-permute-start | bytes 786440 | tf_op jit(solution)/shard_map/ppermute | solution.py:26
  36.6 11.3 %collective-permute-start.17 = (s32[16]{0:T(128)S(1)}, s32[16]{0:T(128)S(1)}, u32[]{:S(2)}, u32[]{:S(2)}) collective-permute-start(s32[16]{0:T(128)S(1)} %pad_add_fusion.refs_5_), channel_id=1, source_target_pairs={{0,1},{1,0},{2,3},{3,2},{4,5},{5,4},{6,7},{7,6},{8,9},{9,8},{10,11... | collective-permute-start | bytes 200 | tf_op jit(solution)/shard_map/ppermute | solution.py:26
  39.3 13.6 %collective-permute-start.10 = (f32[256,256]{1,0:T(8,128)}, f32[256,256]{1,0:T(8,128)S(1)}, u32[]{:S(2)}, u32[]{:S(2)}) collective-permute-start(f32[256,256]{1,0:T(8,128)} %collective-permute-done.9), channel_id=1, source_target_pairs={{0,2},{1,3},{2,4},{3,5},{4,6},{5,7},{6,8},{7,9},{8,10},{9,11},{10,... | collective-permute-start | bytes 786440 | tf_op jit(solution)/shard_map/ppermute | solution.py:26
  40.4 51.6 %collective-permute-start.20 = (f32[6,256,256]{2,1,0:T(8,128)}, f32[6,256,256]{2,1,0:T(8,128)S(1)}, u32[]{:S(2)}, u32[]{:S(2)}) collective-permute-start(f32[6,256,256]{2,1,0:T(8,128)} %bitcast.61), channel_id=1, source_target_pairs={{0,1},{1,0},{2,3},{3,2},{4,5},{5,4},{6,7},{7,6},{8,9},{9,8},{10,11... | collective-permute-start | bytes 4718600 | tf_op jit(solution)/shard_map/ppermute | solution.py:26
  40.5 28.5 %collective-permute-start.1 = (f32[520,256]{1,0:T(8,128)S(1)}, f32[520,256]{1,0:T(8,128)S(1)}, u32[]{:S(2)}, u32[]{:S(2)}) collective-permute-start(f32[520,256]{1,0:T(8,128)S(1)} %collective-permute-done), channel_id=1, source_target_pairs={{0,2},{1,3},{2,4},{3,5},{4,6},{5,7},{6,8},{7,9},{8,10},{9,11},{10,... | collective-permute-start | bytes 1597448 | tf_op jit(solution)/shard_map/ppermute | solution.py:26
  40.6 28.4 %collective-permute-start.4 = (f32[520,256]{1,0:T(8,128)S(1)}, f32[520,256]{1,0:T(8,128)S(1)}, u32[]{:S(2)}, u32[]{:S(2)}) collective-permute-start(f32[520,256]{1,0:T(8,128)S(1)} %collective-permute-done.3), channel_id=1, source_target_pairs={{0,254},{1,255},{2,0},{3,1},{4,2},{5,3},{6,4},{7,5},{8,6},{9,7},{1... | collective-permute-start | bytes 1597448 | tf_op jit(solution)/shard_map/ppermute | solution.py:26
  47.9 66.8 %slice-start.1 = ((s8[6291456]{0:T(1024)(128)(4,1)}), s8[4194304]{0:T(1024)(128)(4,1)S(1)}, s32[]{:S(2)}) async-start(s8[6291456]{0:T(1024)(128)(4,1)} %bitcast.55), calls=%async_computation.1 | async-start | bytes 8388608
  47.9 16.7 %collective-permute-start.26 = (f32[256,256]{1,0:T(8,128)S(1)}, f32[256,256]{1,0:T(8,128)S(1)}, u32[]{:S(2)}, u32[]{:S(2)}) collective-permute-start(f32[256,256]{1,0:T(8,128)S(1)} %get-tuple-element.16), channel_id=1, source_target_pairs={{0,128},{1,129},{2,130},{3,131},{4,132},{5,133},{6,134},{7,135},{8... | collective-permute-start | bytes 786440 | tf_op jit(solution)/shard_map/ppermute | solution.py:26
  52.9 11.6 %collective-permute-start.13 = (f32[256,256]{1,0:T(8,128)}, f32[256,256]{1,0:T(8,128)S(1)}, u32[]{:S(2)}, u32[]{:S(2)}) collective-permute-start(f32[256,256]{1,0:T(8,128)} %collective-permute-done.12), channel_id=1, source_target_pairs={{0,254},{1,255},{2,0},{3,1},{4,2},{5,3},{6,4},{7,5},{8,6},{9,7},{1... | collective-permute-start | bytes 786440 | tf_op jit(solution)/shard_map/ppermute | solution.py:26
  64.5 11.8 %collective-permute-start.24 = (f32[512,256]{1,0:T(8,128)S(1)}, f32[512,256]{1,0:T(8,128)S(1)}, u32[]{:S(2)}, u32[]{:S(2)}) collective-permute-start(f32[512,256]{1,0:T(8,128)S(1)} %pad_maximum_fusion.1.refs_16_.refs_17_), channel_id=1, source_target_pairs={{0,1},{1,0},{2,3},{3,2},{4,5},{5,4},{6,7},{7,6},{8,9},{9,8},{10,11... | collective-permute-start | bytes 1572872 | tf_op jit(solution)/shard_map/ppermute | solution.py:26
  64.6 11.8 %collective-permute-start.14 = (f32[256,256]{1,0:T(8,128)S(1)}, f32[256,256]{1,0:T(8,128)S(1)}, u32[]{:S(2)}, u32[]{:S(2)}) collective-permute-start(f32[256,256]{1,0:T(8,128)S(1)} %get-tuple-element.20), channel_id=1, source_target_pairs={{0,128},{1,129},{2,130},{3,131},{4,132},{5,133},{6,134},{7,135},{8... | collective-permute-start | bytes 786440 | tf_op jit(solution)/shard_map/ppermute | solution.py:26
  69.0 19.7 %collective-permute-start.2 = (f32[520,256]{1,0:T(8,128)S(1)}, f32[520,256]{1,0:T(8,128)S(1)}, u32[]{:S(2)}, u32[]{:S(2)}) collective-permute-start(f32[520,256]{1,0:T(8,128)S(1)} %collective-permute-done.1), channel_id=1, source_target_pairs={{0,2},{1,3},{2,4},{3,5},{4,6},{5,7},{6,8},{7,9},{8,10},{9,11},{10,... | collective-permute-start | bytes 1597448 | tf_op jit(solution)/shard_map/ppermute | solution.py:26
  69.0 19.7 %collective-permute-start.5 = (f32[520,256]{1,0:T(8,128)S(1)}, f32[520,256]{1,0:T(8,128)S(1)}, u32[]{:S(2)}, u32[]{:S(2)}) collective-permute-start(f32[520,256]{1,0:T(8,128)S(1)} %collective-permute-done.4), channel_id=1, source_target_pairs={{0,254},{1,255},{2,0},{3,1},{4,2},{5,3},{6,4},{7,5},{8,6},{9,7},{1... | collective-permute-start | bytes 1597448 | tf_op jit(solution)/shard_map/ppermute | solution.py:26
  76.3 13.6 %collective-permute-start.18 = (f32[520,256]{1,0:T(8,128)S(1)}, f32[520,256]{1,0:T(8,128)S(1)}, u32[]{:S(2)}, u32[]{:S(2)}) collective-permute-start(f32[520,256]{1,0:T(8,128)S(1)} %get-tuple-element.12.refs_14_), channel_id=1, source_target_pairs={{0,1},{1,0},{2,3},{3,2},{4,5},{5,4},{6,7},{7,6},{8,9},{9,8},{10,11... | collective-permute-start | bytes 1597448 | tf_op jit(solution)/shard_map/ppermute | solution.py:26
  76.5 14.5 %collective-permute-start.21 = (f32[520,256]{1,0:T(8,128)S(1)}, f32[520,256]{1,0:T(8,128)S(1)}, u32[]{:S(2)}, u32[]{:S(2)}) collective-permute-start(f32[520,256]{1,0:T(8,128)S(1)} %get-tuple-element.11), channel_id=1, source_target_pairs={{0,128},{1,129},{2,130},{3,131},{4,132},{5,133},{6,134},{7,135},{8... | collective-permute-start | bytes 1597448 | tf_op jit(solution)/shard_map/ppermute | solution.py:26
  77.8 36.9 %copy-start = (f32[1,6,256,256]{3,2,1,0:T(8,128)S(1)}, f32[1,6,256,256]{3,2,1,0:T(8,128)}, u32[]{:S(2)}) copy-start(f32[1,6,256,256]{3,2,1,0:T(8,128)} %param.12) | copy-start | bytes 4718596
  77.8 36.9 %copy-start.1 = (s32[1,24]{1,0:T(1,128)S(1)}, s32[1,24]{1,0:T(1,128)}, u32[]{:S(2)}) copy-start(s32[1,24]{1,0:T(1,128)} %param.10) | copy-start | bytes 292
  77.8 36.9 %copy-start.2 = (s32[1,24]{1,0:T(1,128)S(1)}, s32[1,24]{1,0:T(1,128)}, u32[]{:S(2)}) copy-start(s32[1,24]{1,0:T(1,128)} %param.11) | copy-start | bytes 292
  88.7 3.2 %collective-permute-start.28 = (f32[512,256]{1,0:T(8,128)S(1)}, f32[512,256]{1,0:T(8,128)S(1)}, u32[]{:S(2)}, u32[]{:S(2)}) collective-permute-start(f32[512,256]{1,0:T(8,128)S(1)} %pad_maximum_fusion.2.refs_24_.refs_25_), channel_id=1, source_target_pairs={{0,1},{1,0},{2,3},{3,2},{4,5},{5,4},{6,7},{7,6},{8,9},{9,8},{10,11... | collective-permute-start | bytes 1572872 | tf_op jit(solution)/shard_map/ppermute | solution.py:26
  88.7 15.0 %collective-permute-start.25 = (f32[520,256]{1,0:T(8,128)S(1)}, f32[520,256]{1,0:T(8,128)S(1)}, u32[]{:S(2)}, u32[]{:S(2)}) collective-permute-start(f32[520,256]{1,0:T(8,128)S(1)} %get-tuple-element.9), channel_id=1, source_target_pairs={{0,128},{1,129},{2,130},{3,131},{4,132},{5,133},{6,134},{7,135},{8... | collective-permute-start | bytes 1597448 | tf_op jit(solution)/shard_map/ppermute | solution.py:26
  90.0 13.7 %collective-permute-start.19 = (f32[520,256]{1,0:T(8,128)S(1)}, f32[520,256]{1,0:T(8,128)S(1)}, u32[]{:S(2)}, u32[]{:S(2)}) collective-permute-start(f32[520,256]{1,0:T(8,128)S(1)} %get-tuple-element.10.refs_22_), channel_id=1, source_target_pairs={{0,1},{1,0},{2,3},{3,2},{4,5},{5,4},{6,7},{7,6},{8,9},{9,8},{10,11... | collective-permute-start | bytes 1597448 | tf_op jit(solution)/shard_map/ppermute | solution.py:26
  90.9 23.7 %collective-permute-start.7 = (f32[520,256]{1,0:T(8,128)S(1)}, f32[520,256]{1,0:T(8,128)S(1)}, u32[]{:S(2)}, u32[]{:S(2)}) collective-permute-start(f32[520,256]{1,0:T(8,128)S(1)} %get-tuple-element.13), channel_id=1, source_target_pairs={{0,128},{1,129},{2,130},{3,131},{4,132},{5,133},{6,134},{7,135},{8... | collective-permute-start | bytes 1597448 | tf_op jit(solution)/shard_map/ppermute | solution.py:26
  91.9 22.7 %collective-permute-start.23 = (f32[520,256]{1,0:T(8,128)S(1)}, f32[520,256]{1,0:T(8,128)S(1)}, u32[]{:S(2)}, u32[]{:S(2)}) collective-permute-start(f32[520,256]{1,0:T(8,128)S(1)} %collective-permute-done.21.refs_15_), channel_id=1, source_target_pairs={{0,1},{1,0},{2,3},{3,2},{4,5},{5,4},{6,7},{7,6},{8,9},{9,8},{10,11... | collective-permute-start | bytes 1597448 | tf_op jit(solution)/shard_map/ppermute | solution.py:26
  92.0 29.7 %collective-permute-start.6 = (f32[520,256]{1,0:T(8,128)S(1)}, f32[520,256]{1,0:T(8,128)S(1)}, u32[]{:S(2)}, u32[]{:S(2)}) collective-permute-start(f32[520,256]{1,0:T(8,128)S(1)} %get-tuple-element.14.refs_8_), channel_id=1, source_target_pairs={{0,1},{1,0},{2,3},{3,2},{4,5},{5,4},{6,7},{7,6},{8,9},{9,8},{10,11... | collective-permute-start | bytes 1597448 | tf_op jit(solution)/shard_map/ppermute | solution.py:26
  103.7 11.0 %collective-permute-start.27 = (f32[520,256]{1,0:T(8,128)S(1)}, f32[520,256]{1,0:T(8,128)S(1)}, u32[]{:S(2)}, u32[]{:S(2)}) collective-permute-start(f32[520,256]{1,0:T(8,128)S(1)} %collective-permute-done.25.refs_23_), channel_id=1, source_target_pairs={{0,1},{1,0},{2,3},{3,2},{4,5},{5,4},{6,7},{7,6},{8,9},{9,8},{10,11... | collective-permute-start | bytes 1597448 | tf_op jit(solution)/shard_map/ppermute | solution.py:26
  103.7 18.0 %collective-permute-start.16 = (f32[512,256]{1,0:T(8,128)S(1)}, f32[512,256]{1,0:T(8,128)S(1)}, u32[]{:S(2)}, u32[]{:S(2)}) collective-permute-start(f32[512,256]{1,0:T(8,128)S(1)} %pad_maximum_fusion.refs_10_.refs_11_), channel_id=1, source_target_pairs={{0,1},{1,0},{2,3},{3,2},{4,5},{5,4},{6,7},{7,6},{8,9},{9,8},{10,11... | collective-permute-start | bytes 1572872 | tf_op jit(solution)/shard_map/ppermute | solution.py:26
  114.6 7.1 %collective-permute-start.15 = (f32[520,256]{1,0:T(8,128)S(1)}, f32[520,256]{1,0:T(8,128)S(1)}, u32[]{:S(2)}, u32[]{:S(2)}) collective-permute-start(f32[520,256]{1,0:T(8,128)S(1)} %collective-permute-done.7.refs_9_), channel_id=1, source_target_pairs={{0,1},{1,0},{2,3},{3,2},{4,5},{5,4},{6,7},{7,6},{8,9},{9,8},{10,11... | collective-permute-start | bytes 1597448 | tf_op jit(solution)/shard_map/ppermute | solution.py:26
  123.0 50.8 %collective-permute-start.29 = (f32[8,256,256]{2,1,0:T(8,128)S(1)}, f32[8,256,256]{2,1,0:T(8,128)S(1)}, u32[]{:S(2)}, u32[]{:S(2)}) collective-permute-start(f32[8,256,256]{2,1,0:T(8,128)S(1)} %get-tuple-element.8), channel_id=1, source_target_pairs={{0,128},{1,129},{2,130},{3,131},{4,132},{5,133},{6,134},{7,135},{8... | collective-permute-start | bytes 6291464 | tf_op jit(solution)/shard_map/ppermute | solution.py:26
where the time goes:
time: 177 us; the launch traced here: 175 us
  waiting for transfers between devices  101 us (57%)
  starting transfers between devices  55 us (31%)
  Pallas kernels  8.21 us (5%)
  other arithmetic  7.67 us (4%)
  local copies, waits for them, and re-layouts  2.51 us (1%)
    ppermute x30, waiting for transfers between devices, routed(): return lax.ppermute(value, BOTH, route)  101 us
    ppermute x30, starting transfers between devices, routed(): return lax.ppermute(value, BOTH, route)  55 us
    pallas_call x2, Pallas kernels, multiply(): pl.pallas_call(kernel, out_shape=[part, part] if last else full, in_specs...  8.21 us
  transfers between devices with their start and end apart: 30, of which 10 were waited for; matrix products, arithmetic and copies ran while one was open for 4% of the time, Pallas kernels for 4%

commit v1 on v0

--- a/solution.py
+++ b/solution.py
@@ -1,3 +1,5 @@
+import functools
+
 import jax
 import jax.numpy as jnp
 from jax import lax
@@ -58,33 +60,14 @@
     return dot(a_high, b_high) + (dot(a_high, b_low) + dot(a_low, b_high))
 
 
-def multiply_kernel(
-    n_whole, n_split, first, last, info, a_rows, a_cols, c_rows, c_cols, *refs
-):
-    n_panels = n_whole + n_split
-    notes, a_hbm, refs = refs[:n_panels], refs[n_panels], refs[n_panels + 1 :]
-    whole, refs = refs[:n_whole], refs[n_whole:]
-    pieces, refs = refs[: 4 * n_split], refs[4 * n_split :]
-    if not first:
-        acc_in, refs = refs[0], refs[1:]
-    if last:
-        keep_out, send_out, refs = refs[0], refs[1], refs[2:]
-    else:
-        acc_out, refs = refs[0], refs[1:]
-    acc, a_buf, b_buf, work, hits, count, sems, acc_sem = refs
-    size = a_buf.shape[-1]
-    n_targets = acc.shape[0]
-    half = n_targets // 2
-
-    if not first:
-        load = pltpu.make_async_copy(acc_in, acc, acc_sem.at[0])
-        load.start()
-
-    per_panel = A_SLOTS * PANEL
-    count[0] = 0
-
-    for p in range(n_panels):
+def scan_kernel(n_early, info, a_rows, a_cols, c_rows, c_cols, *refs):
+    notes, (told, *lists) = refs[:-5], refs[-5:]
+    for i in range(told.shape[0]):
+        told[i] = 0
+    for p in range(len(notes)):
         group = info[p]
+        late = int(p >= n_early)
+        work, hits = lists[2 * late], lists[2 * late + 1]
 
         @pl.when(group >= 0)
         def _():
@@ -98,18 +81,55 @@
                     def _():
                         row, col = a_rows[slot], notes[p][PANEL + q]
                         mask = jnp.int32(0)
-                        for t in range(n_targets):
+                        for t in range(c_rows.shape[0]):
                             hit = (c_rows[t] == row) & (c_cols[t] == col)
                             mask = mask + jnp.where(hit, 1 << t, 0)
 
                         @pl.when(mask != 0)
                         def _():
-                            n = count[0]
-                            work[n] = p * per_panel + m * PANEL + q
+                            n = told[1 + late]
+                            work[n] = ((p - late * n_early) * A_SLOTS + m) * PANEL + q
                             hits[n] = mask
-                            count[0] = n + 1
-
-    total = count[0]
+                            told[1 + late] = n + 1
+                            told[0] = told[0] | mask
+
+
+def scan(info, tables, notes, n_early):
+    smem = pl.BlockSpec(memory_space=pltpu.SMEM)
+    sizes = [8] + 2 * [n_early * A_SLOTS * PANEL] + 2 * [(len(notes) - n_early) * A_SLOTS * PANEL]
+    return pl.pallas_call(
+        functools.partial(scan_kernel, n_early),
+        out_shape=[jax.ShapeDtypeStruct((n,), jnp.int32) for n in sizes],
+        in_specs=[smem] * (5 + len(notes)),
+        out_specs=[smem] * 5,
+        compiler_params=pltpu.CompilerParams(vmem_limit_bytes=2**20),
+        name="scan",
+    )(info, *tables, *notes)
+
+
+def multiply_kernel(n_whole, n_split, last, info, told, work, hits, *refs):
+    n_known = info.shape[0] // 2
+    base = n_known - n_split if last else 0
+    if last:
+        theirs, c_rows, c_cols, refs = *refs[:3], refs[3:]
+    a_hbm, refs = refs[0], refs[1:]
+    whole, refs = refs[:n_whole], refs[n_whole:]
+    pieces, refs = refs[: 4 * n_split], refs[4 * n_split :]
+    if last:
+        acc_in, keep_out, send_out, plan, refs = *refs[:4], refs[4:]
+    else:
+        acc_out, refs = refs[0], refs[1:]
+    acc, a_buf, b_buf, sems, acc_sem = refs
+    size = a_buf.shape[-1]
+    n_targets = acc.shape[0]
+    half = n_targets // 2
+
+    if last:
+        load = pltpu.make_async_copy(acc_in, acc, acc_sem.at[0])
+        load.start()
+
+    per_panel = A_SLOTS * PANEL
+    total = told[1 + int(last)]
 
     def fetch_b(source, buf):
         pltpu.make_async_copy(source, b_buf.at[buf], sems.at[1, buf]).start()
@@ -118,7 +138,7 @@
         i = work[n]
         panel = lax.div(i, per_panel)
         rest = lax.rem(i, per_panel)
-        a_slot = info[panel] * A_SLOTS + lax.div(rest, PANEL)
+        a_slot = info[base + panel] * A_SLOTS + lax.div(rest, PANEL)
         q = lax.rem(rest, PANEL)
         pltpu.make_async_copy(a_hbm.at[a_slot], a_buf.at[buf], sems.at[0, buf]).start()
         for p in range(n_whole):
@@ -127,7 +147,7 @@
             def _():
                 fetch_b(whole[p].at[q], buf)
 
-        second = (lax.rem(q, 2) != info[n_panels + panel]).astype(jnp.int32)
+        second = (lax.rem(q, 2) != info[n_known + base + panel]).astype(jnp.int32)
         place = lax.div(q, 2)
         tail = (place == FRONT).astype(jnp.int32)
         which = (panel - n_whole) * 4 + tail * 2 + second
@@ -145,10 +165,10 @@
     def _():
         fetch(0, 0)
 
-    if first:
+    if last:
+        load.wait()
+    else:
         acc[...] = jnp.zeros_like(acc)
-    else:
-        load.wait()
 
     @pl.loop(0, total)
     def _(n):
@@ -170,11 +190,29 @@
                 acc[t] = acc[t] + term
 
     if last:
-        out = pltpu.make_async_copy(acc.at[pl.ds(half, half)], send_out, acc_sem.at[0])
-        out.start()
         kept = pltpu.make_async_copy(acc.at[pl.ds(0, half)], keep_out, acc_sem.at[1])
         kept.start()
-        out.wait()
+        sent, come = jnp.int32(0), jnp.int32(0)
+        for t in range(half):
+            goes = lax.rem(lax.shift_right_logical(told[0], half + t), 2)
+            comes = lax.rem(lax.shift_right_logical(theirs[0], half + t), 2)
+
+            @pl.when(goes == 1)
+            def _():
+                pltpu.make_async_copy(acc.at[half + t], send_out.at[sent], acc_sem.at[0]).start()
+
+            plan[8 + t] = come
+            plan[16 + t] = comes
+            plan[24 + t] = (c_rows[t] == c_cols[t]).astype(jnp.int32)
+            sent, come = sent + goes, come + comes
+        plan[0] = jnp.maximum(jnp.maximum(sent, come), 1) - 1
+        for t in range(1, 8):
+            plan[t] = 0
+
+        @pl.loop(0, sent)
+        def _(n):
+            pltpu.make_async_copy(acc.at[half], send_out.at[n], acc_sem.at[0]).wait()
+
         kept.wait()
     else:
         out = pltpu.make_async_copy(acc, acc_out, acc_sem.at[0])
@@ -182,34 +220,30 @@
         out.wait()
 
 
-def multiply(info, tables, notes, a_blocks, whole, pieces, acc, last, n_targets):
+def multiply(info, found, theirs, a_blocks, whole, pieces, acc, n_targets):
     n_whole, n_split = len(whole), len(pieces) // 4
-    n_panels = n_whole + n_split
     size = a_blocks.shape[-1]
-    first = acc is None
+    last = acc is not None
     smem = pl.BlockSpec(memory_space=pltpu.SMEM)
     anywhere = pl.BlockSpec(memory_space=pl.ANY)
-    stays = pl.BlockSpec(memory_space=pltpu.HBM)
     full = jax.ShapeDtypeStruct((n_targets, size, size), jnp.float32)
     part = jax.ShapeDtypeStruct((n_targets // 2, size, size), jnp.float32)
-    numbers = [info, *tables, *notes]
-    operands = [*numbers, a_blocks, *whole, *pieces] + ([] if first else [acc])
+    plan = jax.ShapeDtypeStruct((32,), jnp.int32)
+    numbers = [info, *found, *theirs]
+    blocks = [a_blocks, *whole, *pieces] + ([acc] if last else [])
 
     def kernel(*refs):
-        multiply_kernel(n_whole, n_split, first, last, *refs)
+        multiply_kernel(n_whole, n_split, last, *refs)
 
     return pl.pallas_call(
         kernel,
-        out_shape=[part, part] if last else full,
-        in_specs=[smem] * len(numbers) + [stays] + [anywhere] * (len(operands) - len(numbers) - 1),
-        out_specs=[anywhere, anywhere] if last else anywhere,
+        out_shape=[part, part, plan] if last else full,
+        in_specs=[smem] * len(numbers) + [anywhere] * len(blocks),
+        out_specs=[anywhere, anywhere, smem] if last else anywhere,
         scratch_shapes=[
             pltpu.VMEM((n_targets, size, size), jnp.float32),
             pltpu.VMEM((2, size, size), jnp.float32),
             pltpu.VMEM((2, size, size), jnp.float32),
-            pltpu.SMEM((n_panels * A_SLOTS * PANEL,), jnp.int32),
-            pltpu.SMEM((n_panels * A_SLOTS * PANEL,), jnp.int32),
-            pltpu.SMEM((1,), jnp.int32),
             pltpu.SemaphoreType.DMA((2, 2)),
             pltpu.SemaphoreType.DMA((2,)),
         ],
@@ -218,7 +252,7 @@
         ),
         compiler_params=pltpu.CompilerParams(vmem_limit_bytes=8 * 2**20),
         name="multiply",
-    )(*operands)
+    )(*numbers, *blocks)
 
 
 def local(a_blocks, a_rows, a_cols, b_blocks, b_rows, b_cols, b_count, c_rows, c_cols):
@@ -258,16 +292,6 @@
 
     side = jnp.where(lower, -1, 1)
     zero = jnp.int32(0)
-
-    def run(stages, whole, acc, last):
-        pieces, notes, groups, lows = [], [], [], []
-        for p, m, g, l in stages:
-            pieces += p
-            notes += m
-            groups += g
-            lows += l
-        info = jnp.stack(groups + lows).astype(jnp.int32)
-        return multiply(info, tables, notes, a_blocks, whole, pieces, acc, last, n_targets)
 
     ups, downs, up_tails, down_tails = [], [], [], []
     for _ in range(1, REACH + 1):
@@ -295,13 +319,72 @@
         groups = [group_of(2 * s * side), group_of(2 * s * side + 1 - 2 * core)]
         pieces = [kept, rest, tails, tails, kept2, rest2, tails2, tails2]
         stages.append((pieces, notes, groups, [low, low]))
-    acc = run(stages[:REACH], [b_blocks, partner], None, False)
-    keep, send = run(stages[REACH:], [], acc, True)
-    summed = keep + other_replica(send)
-    diagonal = (target_rows[:half] == target_cols[:half]).astype(jnp.float32)
-    identity = jnp.eye(size, dtype=jnp.float32)
-    result = 1.5 * diagonal[:, None, None] * identity[None, :, :] - 0.5 * summed
+
+    def of(part, i):
+        return [x for stage in part for x in stage[i]]
+
+    early, late = stages[:REACH], stages[REACH:]
+    info = jnp.stack(of(stages, 2) + of(stages, 3))
+    told, work0, hits0, work1, hits1 = scan(
+        info, tables, of(stages, 1), len(of(early, 1))
+    )
+    theirs = other_replica(told)
+    acc = multiply(
+        info, [told, work0, hits0], [], a_blocks, [b_blocks, partner], of(early, 0), None, n_targets
+    )
+    keep, send, plan = multiply(
+        info,
+        [told, work1, hits1],
+        [theirs, target_rows, target_cols],
+        a_blocks,
+        [],
+        of(late, 0),
+        acc,
+        n_targets,
+    )
+    result = lax.switch(
+        plan[0], [functools.partial(finish, n + 1) for n in range(half)], keep, send, plan
+    )
     return result[None]
+
+
+def finish_kernel(plan, keep, come, out):
+    t = pl.program_id(0)
+    size = out.shape[-1]
+    row = lax.broadcasted_iota(jnp.int32, (size, size), 0)
+    col = lax.broadcasted_iota(jnp.int32, (size, size), 1)
+    unit = jnp.where((row == col) & (plan[24 + t] == 1), 1.5, 0.0)
+
+    @pl.when(plan[16 + t] == 1)
+    def _():
+        out[...] = unit - 0.5 * (keep[...] + come[...])
+
+    @pl.when(plan[16 + t] == 0)
+    def _():
+        out[...] = unit - 0.5 * keep[...]
+
+
+def finish(many, keep, send, plan):
+    half, size = keep.shape[0], keep.shape[-1]
+    come = other_replica(send[:many])
+    block = (None, size, size)
+    return pl.pallas_call(
+        finish_kernel,
+        out_shape=jax.ShapeDtypeStruct(keep.shape, jnp.float32),
+        grid_spec=pltpu.PrefetchScalarGridSpec(
+            num_scalar_prefetch=1,
+            grid=(half,),
+            in_specs=[
+                pl.BlockSpec(block, lambda t, plan: (t, 0, 0)),
+                pl.BlockSpec(block, lambda t, plan: (jnp.minimum(plan[8 + t], many - 1), 0, 0)),
+            ],
+            out_specs=pl.BlockSpec(block, lambda t, plan: (t, 0, 0)),
+        ),
+        compiler_params=pltpu.CompilerParams(
+            dimension_semantics=("arbitrary",), vmem_limit_bytes=4 * 2**20
+        ),
+        name="finish",
+    )(plan, keep, come)
 
 
 def solution(mesh):

time: 177 us -> 167 us (0.944)
  the two profiles are of different devices: /device:TPU:8 before, /device:TPU:2 now
where the time goes in v1:
time: 167 us
  waiting for transfers between devices  96.7 us (58%)
  starting transfers between devices  48.4 us (29%)
  Pallas kernels  10.4 us (6%)
  other arithmetic  6.05 us (4%)
  local copies, waits for them, and re-layouts  3.93 us (2%)
    ppermute x31, waiting for transfers between devices, routed(): return lax.ppermute(value, BOTH, route)  96.7 us
    ppermute x31, starting transfers between devices, routed(): return lax.ppermute(value, BOTH, route)  48.4 us
    pallas_call x2, Pallas kernels, multiply(): pl.pallas_call(kernel, out_shape=[part, part, plan] if last else full, in...  5.66 us
    pallas_call x1, Pallas kernels, scan(): pl.pallas_call(functools.partial(scan_kernel, n_early), out_shape=[jax.Sh...  3.66 us
  transfers between devices with their start and end apart: 31, of which 12 were waited for; matrix products, arithmetic and copies ran while one was open for 3% of the time, Pallas kernels for 4%

profile of v1, /device:TPU:2, one launch (start us, length us, event | category | flops | bytes accessed | tf_op | source)
XLA Modules:
  0.0 166.9 jit_solution(4802679023896805151)
XLA Ops:
  0.7 1.2 constant_dynamic-slice_fusion
  2.0 0.8 fusion.1
  2.7 0.8 select_maximum_fusion
  3.6 1.9 %collective-permute-start.9 = (f32[520,256]{1,0:T(8,128)}, f32[520,256]{1,0:T(8,128)S(1)}, u32[]{:S(2)}, u32[]{:S(2)}) collective-permute-start(f32[520,256]{1,0:T(8,128)} %select_maximum_fusion), channel_id=1, source_target_pairs={{0,2},{1,3},{2,4},{3,5},{4,6},{5,7},{6,8},{7,9},{8,10},{9,11},{10,... | collective-permute-start | bytes 1597448 | tf_op jit(solution)/shard_map/ppermute | solution.py:28
  5.5 6.4 %collective-permute-start.10 = (f32[520,256]{1,0:T(8,128)}, f32[520,256]{1,0:T(8,128)S(1)}, u32[]{:S(2)}, u32[]{:S(2)}) collective-permute-start(f32[520,256]{1,0:T(8,128)} %select_maximum_fusion), channel_id=1, source_target_pairs={{0,254},{1,255},{2,0},{3,1},{4,2},{5,3},{6,4},{7,5},{8,6},{9,7},{1... | collective-permute-start | bytes 1597448 | tf_op jit(solution)/shard_map/ppermute | solution.py:28
  11.8 1.0 dynamic-slice_bitcast_fusion
  12.8 0.1 collective-permute-start.20
  12.9 6.2 %collective-permute-start.23 = (f32[256,256]{1,0:T(8,128)S(1)}, f32[256,256]{1,0:T(8,128)}, u32[]{:S(2)}, u32[]{:S(2)}) collective-permute-start(f32[256,256]{1,0:T(8,128)S(1)} %dynamic-slice_bitcast_fusion), channel_id=1, source_target_pairs={{0,254},{1,255},{2,0},{3,1},{4,2},{5,3},{6,4},{7,5},{8,6},{9,7},{1... | collective-permute-start | bytes 786440 | tf_op jit(solution)/shard_map/ppermute | solution.py:28
  19.4 10.5 %collective-permute-done.20 = f32[256,256]{1,0:T(8,128)} collective-permute-done((f32[256,256]{1,0:T(8,128)S(1)}, f32[256,256]{1,0:T(8,128)}, u32[]{:S(2)}, u32[]{:S(2)}) %collective-permute-start.20) | collective-permute-done | bytes 262176 | tf_op jit(solution)/shard_map/ppermute | solution.py:28
  29.9 6.2 %collective-permute-start.24 = (f32[256,256]{1,0:T(8,128)}, f32[256,256]{1,0:T(8,128)}, u32[]{:S(2)}, u32[]{:S(2)}) collective-permute-start(f32[256,256]{1,0:T(8,128)} %collective-permute-done.23), channel_id=1, source_target_pairs={{0,254},{1,255},{2,0},{3,1},{4,2},{5,3},{6,4},{7,5},{8,6},{9,7},{1... | collective-permute-start | bytes 786440 | tf_op jit(solution)/shard_map/ppermute | solution.py:28
  36.1 1.8 %broadcast_select_fusion.9 = (f32[256,256]{1,0:T(8,128)S(1)}, f32[256,256]{1,0:T(8,128)}) fusion(f32[256,256]{1,0:T(8,128)} %collective-permute-done.20, f32[256,256]{1,0:T(8,128)} %collective-permute-done.23, pred[]{:T(512)S(6)} %eq.6), kind=kLoop, calls=%fused_computation.15 | loop fusion | flops 131072 | bytes 1048577 | tf_op jit(solution)/shard_map/jit(_where)/select_n | solution.py:311
  38.1 0.1 stack.50.info.refs_0_
  38.2 0.1 collective-permute-start.12
  38.3 3.6 %collective-permute-done.21 = f32[256,256]{1,0:T(8,128)} collective-permute-done((f32[256,256]{1,0:T(8,128)}, f32[256,256]{1,0:T(8,128)}, u32[]{:S(2)}, u32[]{:S(2)}) %collective-permute-start.21) | collective-permute-done | bytes 262176 | tf_op jit(solution)/shard_map/ppermute | solution.py:28
  41.9 1.1 broadcast_select_fusion.7
  43.0 0.1 collective-permute-start.35
  43.1 0.1 collective-permute-start.22
  43.1 3.0 %collective-permute-done.31 = f32[256,256]{1,0:T(8,128)} collective-permute-done((f32[256,256]{1,0:T(8,128)}, f32[256,256]{1,0:T(8,128)}, u32[]{:S(2)}, u32[]{:S(2)}) %collective-permute-start.31) | collective-permute-done | bytes 262176 | tf_op jit(solution)/shard_map/ppermute | solution.py:28
  46.1 3.2 %collective-permute-start.25 = (f32[256,256]{1,0:T(8,128)}, f32[256,256]{1,0:T(8,128)S(1)}, u32[]{:S(2)}, u32[]{:S(2)}) collective-permute-start(f32[256,256]{1,0:T(8,128)} %collective-permute-done.24), channel_id=1, source_target_pairs={{0,254},{1,255},{2,0},{3,1},{4,2},{5,3},{6,4},{7,5},{8,6},{9,7},{1... | collective-permute-start | bytes 786440 | tf_op jit(solution)/shard_map/ppermute | solution.py:28
  49.4 1.7 %collective-permute-start.13 = (f32[520,256]{1,0:T(8,128)S(1)}, f32[520,256]{1,0:T(8,128)S(1)}, u32[]{:S(2)}, u32[]{:S(2)}) collective-permute-start(f32[520,256]{1,0:T(8,128)S(1)} %collective-permute-done.10), channel_id=1, source_target_pairs={{0,254},{1,255},{2,0},{3,1},{4,2},{5,3},{6,4},{7,5},{8,6},{9,7},{1... | collective-permute-start | bytes 1597448 | tf_op jit(solution)/shard_map/ppermute | solution.py:28
  51.1 1.1 pad_maximum_fusion.1.refs_9_.refs_10_
  52.3 8.5 %collective-permute-done.22 = f32[256,256]{1,0:T(8,128)S(1)} collective-permute-done((f32[256,256]{1,0:T(8,128)}, f32[256,256]{1,0:T(8,128)S(1)}, u32[]{:S(2)}, u32[]{:S(2)}) %collective-permute-start.22) | collective-permute-done | bytes 262176 | tf_op jit(solution)/shard_map/ppermute | solution.py:28
  60.9 0.6 collective-permute-start.8
  61.5 3.4 %collective-permute-done.13 = f32[520,256]{1,0:T(8,128)S(1)} collective-permute-done((f32[520,256]{1,0:T(8,128)S(1)}, f32[520,256]{1,0:T(8,128)S(1)}, u32[]{:S(2)}, u32[]{:S(2)}) %collective-permute-start.13) | collective-permute-done | bytes 532512 | tf_op jit(solution)/shard_map/ppermute | solution.py:28
  64.9 6.7 %collective-permute-start.16 = (f32[520,256]{1,0:T(8,128)S(1)}, f32[520,256]{1,0:T(8,128)S(1)}, u32[]{:S(2)}, u32[]{:S(2)}) collective-permute-start(f32[520,256]{1,0:T(8,128)S(1)} %collective-permute-done.13), channel_id=1, source_target_pairs={{0,254},{1,255},{2,0},{3,1},{4,2},{5,3},{6,4},{7,5},{8,6},{9,7},{1... | collective-permute-start | bytes 1597448 | tf_op jit(solution)/shard_map/ppermute | solution.py:28
  71.6 0.3 collective-permute-start.29
  72.0 0.6 collective-permute-start.11
  72.5 7.0 %collective-permute-done.15 = f32[520,256]{1,0:T(8,128)S(1)} collective-permute-done((f32[520,256]{1,0:T(8,128)S(1)}, f32[520,256]{1,0:T(8,128)S(1)}, u32[]{:S(2)}, u32[]{:S(2)}) %collective-permute-start.15) | collective-permute-done | bytes 532512 | tf_op jit(solution)/shard_map/ppermute | solution.py:28
  79.7 0.7 collective-permute-done.16
  80.4 11.8 %collective-permute-done.26 = f32[256,256]{1,0:T(8,128)S(1)} collective-permute-done((f32[256,256]{1,0:T(8,128)S(1)}, f32[256,256]{1,0:T(8,128)S(1)}, u32[]{:S(2)}, u32[]{:S(2)}) %collective-permute-start.26) | collective-permute-done | bytes 262176 | tf_op jit(solution)/shard_map/ppermute | solution.py:28
  92.3 0.3 collective-permute-start.34
  92.6 0.3 collective-permute-start.17
  92.9 1.7 collective-permute-start.19
  94.6 0.1 collective-permute-start.28
  94.7 12.5 %collective-permute-done.34.refs_16_ = f32[520,256]{1,0:T(8,128)S(1)} collective-permute-done((f32[520,256]{1,0:T(8,128)S(1)}, f32[520,256]{1,0:T(8,128)S(1)}, u32[]{:S(2)}, u32[]{:S(2)}) %collective-permute-start.34) | collective-permute-done | bytes 532512 | tf_op jit(solution)/shard_map/ppermute | solution.py:28
  107.2 0.5 collective-permute-start.36
  107.8 10.4 %collective-permute-done.19.refs_9_ = f32[520,256]{1,0:T(8,128)S(1)} collective-permute-done((f32[520,256]{1,0:T(8,128)S(1)}, f32[520,256]{1,0:T(8,128)S(1)}, u32[]{:S(2)}, u32[]{:S(2)}) %collective-permute-start.19) | collective-permute-done | bytes 532512 | tf_op jit(solution)/shard_map/ppermute | solution.py:28
  118.2 3.7 %scan.1 = (s32[8]{0:T(128)S(1)}, s32[144]{0:T(256)S(1)}, s32[144]{0:T(256)S(1)}, s32[48]{0:T(128)S(1)}, s32[48]{0:T(128)S(1)}) custom-call(s32[16]{0:T(128)S(1)} %stack.50.info.refs_0_, s32[24]{0:T(128)S(1)} %bitcast.71, s32[24]{0:T(128)S(1)} %bitcast.72, s32[16]{0:T(128)S(1)} %get-tuple-element.121.c_rows.refs_5_, s32[16]{0:T(128)S(1)} %get-tuple-element.120.c_cols.refs_6_, ...), custom_call_target="tpu_custom_call" | custom-call | tf_op jit(solution)/shard_map/scan/pallas_call | solution.py:100
  121.9 0.3 collective-permute-start.18
  122.3 2.6 %multiply.2.refs_16_ = f32[16,256,256]{2,1,0:T(8,128)S(1)} custom-call(s32[16]{0:T(128)S(1)} %stack.50.info.refs_0_, s32[8]{0:T(128)S(1)} %get-tuple-element.95.refs_1_, s32[144]{0:T(256)S(1)} %get-tuple-element.98.refs_2_, s32[144]{0:T(256)S(1)} %get-tuple-element.99.refs_3_, f32[24,256,256]{2,1,0:T(8,128)S(1)} %bitcast.65, f32[6,256,256]{2,1,0:T(8,128)S(1)} %bitcast.70, ...), custom_call_target="tpu_custom_call" | custom-call | flops 268435456 | bytes 12582912 | tf_op jit(solution)/shard_map/multiply/pallas_call | solution.py:238
  124.9 0.7 collective-permute-done.18.refs_4_
  125.6 3.1 %multiply.3 = (f32[8,256,256]{2,1,0:T(8,128)S(1)}, f32[8,256,256]{2,1,0:T(8,128)S(1)}, s32[32]{0:T(128)S(1)}) custom-call(s32[16]{0:T(128)S(1)} %stack.50.info.refs_0_, s32[8]{0:T(128)S(1)} %get-tuple-element.95.refs_1_, s32[48]{0:T(128)S(1)} %get-tuple-element.96.refs_2_, s32[48]{0:T(128)S(1)} %get-tuple-element.97.refs_3_, ...), custom_call_target="tpu_custom_call" | custom-call | flops 268435456 | bytes 12582912 | tf_op jit(solution)/shard_map/multiply/pallas_call | solution.py:238
  128.7 36.9 %conditional.1 = (f32[1,8,256,256]{3,2,1,0:T(8,128)S(1)}) conditional(s32[]{:T(128)} %bitcast.41, (f32[8,256,256]{2,1,0:T(8,128)S(1)}, s32[32]{0:T(128)S(1)}, f32[8,256,256]{2,1,0:T(8,128)S(1)}) %tuple.37, (f32[8,256,256]{2,1,0:T(8,128)S(1)}, s32[32]{0:T(128)S(1)}, f32[8,256,256]{2,1,0:T(8,128)S(1)}) %tuple.37, ...), branch_computations={%region_0.1_spmd, %region_1.2_spmd, %region_2.3_spmd, %region_3.4_... | conditional | bytes 11010096 | solution.py:345
  128.9 0.1 slice.56
  129.1 11.0 %collective-permute-start.4 = (f32[5,256,256]{2,1,0:T(8,128)S(1)}, f32[5,256,256]{2,1,0:T(8,128)S(1)}, u32[]{:S(2)}, u32[]{:S(2)}) collective-permute-start(f32[5,256,256]{2,1,0:T(8,128)S(1)} %slice.56), channel_id=1, source_target_pairs={{0,128},{1,129},{2,130},{3,131},{4,132},{5,133},{6,134},{7,135},{8... | collective-permute-start | bytes 3932168 | tf_op jit(solution)/shard_map/cond/branch_4_fun/ppermute | solution.py:28
  140.0 24.5 %collective-permute-done.4.come = f32[5,256,256]{2,1,0:T(8,128)S(1)} collective-permute-done((f32[5,256,256]{2,1,0:T(8,128)S(1)}, f32[5,256,256]{2,1,0:T(8,128)S(1)}, u32[]{:S(2)}, u32[]{:S(2)}) %collective-permute-start.4) | collective-permute-done | bytes 1310752 | tf_op jit(solution)/shard_map/cond/branch_4_fun/ppermute | solution.py:28
  164.5 1.1 finish.12
  165.6 1.3 copy-done.3
  (67 shorter events, 0.8 us)
Async XLA Ops:
  0.0 37.9 %copy-start.7 = (s32[1,6]{1,0:T(1,128)S(1)}, s32[1,6]{1,0:T(1,128)}, u32[]{:S(2)}) copy-start(s32[1,6]{1,0:T(1,128)} %param.21) | copy-start | bytes 76
  0.0 37.9 %copy-start.6 = (s32[1,6]{1,0:T(1,128)S(1)}, s32[1,6]{1,0:T(1,128)}, u32[]{:S(2)}) copy-start(s32[1,6]{1,0:T(1,128)} %param.22) | copy-start | bytes 76
  0.0 19.1 %copy-start.4 = (s32[1,16]{1,0:T(1,128)S(1)}, s32[1,16]{1,0:T(1,128)}, u32[]{:S(2)}) copy-start(s32[1,16]{1,0:T(1,128)} %param.25) | copy-start | bytes 196
  0.0 19.2 %copy-start.5 = (s32[1,16]{1,0:T(1,128)S(1)}, s32[1,16]{1,0:T(1,128)}, u32[]{:S(2)}) copy-start(s32[1,16]{1,0:T(1,128)} %param.24) | copy-start | bytes 196
  0.7 121.5 %slice-start = ((s8[6291456]{0:T(1024)(128)(4,1)}), s8[2097152]{0:T(1024)(128)(4,1)S(1)}, s32[]{:S(2)}) async-start(s8[6291456]{0:T(1024)(128)(4,1)} %bitcast.63), calls=%async_computation | async-start | bytes 4194304
  3.6 34.6 %collective-permute-start.9 = (f32[520,256]{1,0:T(8,128)}, f32[520,256]{1,0:T(8,128)S(1)}, u32[]{:S(2)}, u32[]{:S(2)}) collective-permute-start(f32[520,256]{1,0:T(8,128)} %select_maximum_fusion), channel_id=1, source_target_pairs={{0,2},{1,3},{2,4},{3,5},{4,6},{5,7},{6,8},{7,9},{8,10},{9,11},{10,... | collective-permute-start | bytes 1597448 | tf_op jit(solution)/shard_map/ppermute | solution.py:28
  5.5 43.9 %collective-permute-start.10 = (f32[520,256]{1,0:T(8,128)}, f32[520,256]{1,0:T(8,128)S(1)}, u32[]{:S(2)}, u32[]{:S(2)}) collective-permute-start(f32[520,256]{1,0:T(8,128)} %select_maximum_fusion), channel_id=1, source_target_pairs={{0,254},{1,255},{2,0},{3,1},{4,2},{5,3},{6,4},{7,5},{8,6},{9,7},{1... | collective-permute-start | bytes 1597448 | tf_op jit(solution)/shard_map/ppermute | solution.py:28
  12.8 17.1 %collective-permute-start.20 = (f32[256,256]{1,0:T(8,128)S(1)}, f32[256,256]{1,0:T(8,128)}, u32[]{:S(2)}, u32[]{:S(2)}) collective-permute-start(f32[256,256]{1,0:T(8,128)S(1)} %dynamic-slice_bitcast_fusion), channel_id=1, source_target_pairs={{0,2},{1,3},{2,4},{3,5},{4,6},{5,7},{6,8},{7,9},{8,10},{9,11},{10,... | collective-permute-start | bytes 786440 | tf_op jit(solution)/shard_map/ppermute | solution.py:28
  12.9 17.0 %collective-permute-start.23 = (f32[256,256]{1,0:T(8,128)S(1)}, f32[256,256]{1,0:T(8,128)}, u32[]{:S(2)}, u32[]{:S(2)}) collective-permute-start(f32[256,256]{1,0:T(8,128)S(1)} %dynamic-slice_bitcast_fusion), channel_id=1, source_target_pairs={{0,254},{1,255},{2,0},{3,1},{4,2},{5,3},{6,4},{7,5},{8,6},{9,7},{1... | collective-permute-start | bytes 786440 | tf_op jit(solution)/shard_map/ppermute | solution.py:28
  29.9 12.0 %collective-permute-start.21 = (f32[256,256]{1,0:T(8,128)}, f32[256,256]{1,0:T(8,128)}, u32[]{:S(2)}, u32[]{:S(2)}) collective-permute-start(f32[256,256]{1,0:T(8,128)} %collective-permute-done.20), channel_id=1, source_target_pairs={{0,2},{1,3},{2,4},{3,5},{4,6},{5,7},{6,8},{7,9},{8,10},{9,11},{10,... | collective-permute-start | bytes 786440 | tf_op jit(solution)/shard_map/ppermute | solution.py:28
  29.9 12.0 %collective-permute-start.24 = (f32[256,256]{1,0:T(8,128)}, f32[256,256]{1,0:T(8,128)}, u32[]{:S(2)}, u32[]{:S(2)}) collective-permute-start(f32[256,256]{1,0:T(8,128)} %collective-permute-done.23), channel_id=1, source_target_pairs={{0,254},{1,255},{2,0},{3,1},{4,2},{5,3},{6,4},{7,5},{8,6},{9,7},{1... | collective-permute-start | bytes 786440 | tf_op jit(solution)/shard_map/ppermute | solution.py:28
  37.9 8.2 %collective-permute-start.31 = (f32[256,256]{1,0:T(8,128)}, f32[256,256]{1,0:T(8,128)}, u32[]{:S(2)}, u32[]{:S(2)}) collective-permute-start(f32[256,256]{1,0:T(8,128)} %get-tuple-element.113), channel_id=1, source_target_pairs={{0,128},{1,129},{2,130},{3,131},{4,132},{5,133},{6,134},{7,135},{8... | collective-permute-start | bytes 786440 | tf_op jit(solution)/shard_map/ppermute | solution.py:28
  38.2 22.6 %collective-permute-start.12 = (f32[520,256]{1,0:T(8,128)S(1)}, f32[520,256]{1,0:T(8,128)S(1)}, u32[]{:S(2)}, u32[]{:S(2)}) collective-permute-start(f32[520,256]{1,0:T(8,128)S(1)} %collective-permute-done.9), channel_id=1, source_target_pairs={{0,2},{1,3},{2,4},{3,5},{4,6},{5,7},{6,8},{7,9},{8,10},{9,11},{10,... | collective-permute-start | bytes 1597448 | tf_op jit(solution)/shard_map/ppermute | solution.py:28
  43.0 28.6 %collective-permute-start.35 = (f32[256,256]{1,0:T(8,128)S(1)}, f32[256,256]{1,0:T(8,128)S(1)}, u32[]{:S(2)}, u32[]{:S(2)}) collective-permute-start(f32[256,256]{1,0:T(8,128)S(1)} %get-tuple-element.111), channel_id=1, source_target_pairs={{0,128},{1,129},{2,130},{3,131},{4,132},{5,133},{6,134},{7,135},{8... | collective-permute-start | bytes 786440 | tf_op jit(solution)/shard_map/ppermute | solution.py:28
  43.1 17.8 %collective-permute-start.22 = (f32[256,256]{1,0:T(8,128)}, f32[256,256]{1,0:T(8,128)S(1)}, u32[]{:S(2)}, u32[]{:S(2)}) collective-permute-start(f32[256,256]{1,0:T(8,128)} %collective-permute-done.21), channel_id=1, source_target_pairs={{0,2},{1,3},{2,4},{3,5},{4,6},{5,7},{6,8},{7,9},{8,10},{9,11},{10,... | collective-permute-start | bytes 786440 | tf_op jit(solution)/shard_map/ppermute | solution.py:28
  46.1 14.7 %collective-permute-start.25 = (f32[256,256]{1,0:T(8,128)}, f32[256,256]{1,0:T(8,128)S(1)}, u32[]{:S(2)}, u32[]{:S(2)}) collective-permute-start(f32[256,256]{1,0:T(8,128)} %collective-permute-done.24), channel_id=1, source_target_pairs={{0,254},{1,255},{2,0},{3,1},{4,2},{5,3},{6,4},{7,5},{8,6},{9,7},{1... | collective-permute-start | bytes 786440 | tf_op jit(solution)/shard_map/ppermute | solution.py:28
  49.4 15.5 %collective-permute-start.13 = (f32[520,256]{1,0:T(8,128)S(1)}, f32[520,256]{1,0:T(8,128)S(1)}, u32[]{:S(2)}, u32[]{:S(2)}) collective-permute-start(f32[520,256]{1,0:T(8,128)S(1)} %collective-permute-done.10), channel_id=1, source_target_pairs={{0,254},{1,255},{2,0},{3,1},{4,2},{5,3},{6,4},{7,5},{8,6},{9,7},{1... | collective-permute-start | bytes 1597448 | tf_op jit(solution)/shard_map/ppermute | solution.py:28
  51.1 20.5 %copy-start = (f32[1,6,256,256]{3,2,1,0:T(8,128)S(1)}, f32[1,6,256,256]{3,2,1,0:T(8,128)}, u32[]{:S(2)}) copy-start(f32[1,6,256,256]{3,2,1,0:T(8,128)} %param.20) | copy-start | bytes 4718596
  52.2 70.0 %slice-start.1 = ((s8[6291456]{0:T(1024)(128)(4,1)}), s8[4194304]{0:T(1024)(128)(4,1)S(1)}, s32[]{:S(2)}) async-start(s8[6291456]{0:T(1024)(128)(4,1)} %bitcast.63), calls=%async_computation.1 | async-start | bytes 8388608
  60.8 11.7 %collective-permute-start.33 = (f32[512,256]{1,0:T(8,128)S(1)}, f32[512,256]{1,0:T(8,128)S(1)}, u32[]{:S(2)}, u32[]{:S(2)}) collective-permute-start(f32[512,256]{1,0:T(8,128)S(1)} %pad_maximum_fusion.1.refs_9_.refs_10_), channel_id=1, source_target_pairs={{0,1},{1,0},{2,3},{3,2},{4,5},{5,4},{6,7},{7,6},{8,9},{9,8},{10,11... | collective-permute-start | bytes 1572872 | tf_op jit(solution)/shard_map/ppermute | solution.py:28
  60.8 18.7 %collective-permute-start.15 = (f32[520,256]{1,0:T(8,128)S(1)}, f32[520,256]{1,0:T(8,128)S(1)}, u32[]{:S(2)}, u32[]{:S(2)}) collective-permute-start(f32[520,256]{1,0:T(8,128)S(1)} %collective-permute-done.12), channel_id=1, source_target_pairs={{0,2},{1,3},{2,4},{3,5},{4,6},{5,7},{6,8},{7,9},{8,10},{9,11},{10,... | collective-permute-start | bytes 1597448 | tf_op jit(solution)/shard_map/ppermute | solution.py:28
  60.9 11.1 %collective-permute-start.8 = (s32[16]{0:T(128)S(1)}, s32[16]{0:T(128)S(1)}, u32[]{:S(2)}, u32[]{:S(2)}) collective-permute-start(s32[16]{0:T(128)S(1)} %pad_add_fusion.refs_0_), channel_id=1, source_target_pairs={{0,1},{1,0},{2,3},{3,2},{4,5},{5,4},{6,7},{7,6},{8,9},{9,8},{10,11... | collective-permute-start | bytes 200 | tf_op jit(solution)/shard_map/ppermute | solution.py:28
  64.9 15.5 %collective-permute-start.16 = (f32[520,256]{1,0:T(8,128)S(1)}, f32[520,256]{1,0:T(8,128)S(1)}, u32[]{:S(2)}, u32[]{:S(2)}) collective-permute-start(f32[520,256]{1,0:T(8,128)S(1)} %collective-permute-done.13), channel_id=1, source_target_pairs={{0,254},{1,255},{2,0},{3,1},{4,2},{5,3},{6,4},{7,5},{8,6},{9,7},{1... | collective-permute-start | bytes 1597448 | tf_op jit(solution)/shard_map/ppermute | solution.py:28
  71.6 50.3 %collective-permute-start.29 = (f32[6,256,256]{2,1,0:T(8,128)S(1)}, f32[6,256,256]{2,1,0:T(8,128)S(1)}, u32[]{:S(2)}, u32[]{:S(2)}) collective-permute-start(f32[6,256,256]{2,1,0:T(8,128)S(1)} %bitcast.69), channel_id=1, source_target_pairs={{0,1},{1,0},{2,3},{3,2},{4,5},{5,4},{6,7},{7,6},{8,9},{9,8},{10,11... | collective-permute-start | bytes 4718600 | tf_op jit(solution)/shard_map/ppermute | solution.py:28
  72.0 20.3 %collective-permute-start.11 = (f32[520,256]{1,0:T(8,128)S(1)}, f32[520,256]{1,0:T(8,128)S(1)}, u32[]{:S(2)}, u32[]{:S(2)}) collective-permute-start(f32[520,256]{1,0:T(8,128)S(1)} %get-tuple-element.107.refs_7_), channel_id=1, source_target_pairs={{0,1},{1,0},{2,3},{3,2},{4,5},{5,4},{6,7},{7,6},{8,9},{9,8},{10,11... | collective-permute-start | bytes 1597448 | tf_op jit(solution)/shard_map/ppermute | solution.py:28
  72.5 20.0 %collective-permute-start.30 = (f32[520,256]{1,0:T(8,128)S(1)}, f32[520,256]{1,0:T(8,128)S(1)}, u32[]{:S(2)}, u32[]{:S(2)}) collective-permute-start(f32[520,256]{1,0:T(8,128)S(1)} %get-tuple-element.106), channel_id=1, source_target_pairs={{0,128},{1,129},{2,130},{3,131},{4,132},{5,133},{6,134},{7,135},{8... | collective-permute-start | bytes 1597448 | tf_op jit(solution)/shard_map/ppermute | solution.py:28
  79.6 13.3 %collective-permute-start.37 = (f32[512,256]{1,0:T(8,128)S(1)}, f32[512,256]{1,0:T(8,128)S(1)}, u32[]{:S(2)}, u32[]{:S(2)}) collective-permute-start(f32[512,256]{1,0:T(8,128)S(1)} %pad_maximum_fusion.2.refs_17_.refs_18_), channel_id=1, source_target_pairs={{0,1},{1,0},{2,3},{3,2},{4,5},{5,4},{6,7},{7,6},{8,9},{9,8},{10,11... | collective-permute-start | bytes 1572872 | tf_op jit(solution)/shard_map/ppermute | solution.py:28
  79.6 38.6 %copy-start.1 = (s32[1,24]{1,0:T(1,128)S(1)}, s32[1,24]{1,0:T(1,128)}, u32[]{:S(2)}) copy-start(s32[1,24]{1,0:T(1,128)} %param.18) | copy-start | bytes 292
  79.7 38.6 %copy-start.2 = (s32[1,24]{1,0:T(1,128)S(1)}, s32[1,24]{1,0:T(1,128)}, u32[]{:S(2)}) copy-start(s32[1,24]{1,0:T(1,128)} %param.19) | copy-start | bytes 292
  80.3 11.9 %collective-permute-start.26 = (f32[256,256]{1,0:T(8,128)S(1)}, f32[256,256]{1,0:T(8,128)S(1)}, u32[]{:S(2)}, u32[]{:S(2)}) collective-permute-start(f32[256,256]{1,0:T(8,128)S(1)} %get-tuple-element.115), channel_id=1, source_target_pairs={{0,128},{1,129},{2,130},{3,131},{4,132},{5,133},{6,134},{7,135},{8... | collective-permute-start | bytes 786440 | tf_op jit(solution)/shard_map/ppermute | solution.py:28
  92.3 2.3 %collective-permute-start.14 = (f32[520,256]{1,0:T(8,128)S(1)}, f32[520,256]{1,0:T(8,128)S(1)}, u32[]{:S(2)}, u32[]{:S(2)}) collective-permute-start(f32[520,256]{1,0:T(8,128)S(1)} %get-tuple-element.105.refs_15_), channel_id=1, source_target_pairs={{0,1},{1,0},{2,3},{3,2},{4,5},{5,4},{6,7},{7,6},{8,9},{9,8},{10,11... | collective-permute-start | bytes 1597448 | tf_op jit(solution)/shard_map/ppermute | solution.py:28
  92.3 15.0 %collective-permute-start.34 = (f32[520,256]{1,0:T(8,128)S(1)}, f32[520,256]{1,0:T(8,128)S(1)}, u32[]{:S(2)}, u32[]{:S(2)}) collective-permute-start(f32[520,256]{1,0:T(8,128)S(1)} %get-tuple-element.104), channel_id=1, source_target_pairs={{0,128},{1,129},{2,130},{3,131},{4,132},{5,133},{6,134},{7,135},{8... | collective-permute-start | bytes 1597448 | tf_op jit(solution)/shard_map/ppermute | solution.py:28
  92.6 14.7 %collective-permute-start.17 = (f32[520,256]{1,0:T(8,128)S(1)}, f32[520,256]{1,0:T(8,128)S(1)}, u32[]{:S(2)}, u32[]{:S(2)}) collective-permute-start(f32[520,256]{1,0:T(8,128)S(1)} %get-tuple-element.109.refs_8_), channel_id=1, source_target_pairs={{0,1},{1,0},{2,3},{3,2},{4,5},{5,4},{6,7},{7,6},{8,9},{9,8},{10,11... | collective-permute-start | bytes 1597448 | tf_op jit(solution)/shard_map/ppermute | solution.py:28
  92.9 25.3 %collective-permute-start.19 = (f32[520,256]{1,0:T(8,128)S(1)}, f32[520,256]{1,0:T(8,128)S(1)}, u32[]{:S(2)}, u32[]{:S(2)}) collective-permute-start(f32[520,256]{1,0:T(8,128)S(1)} %get-tuple-element.108), channel_id=1, source_target_pairs={{0,128},{1,129},{2,130},{3,131},{4,132},{5,133},{6,134},{7,135},{8... | collective-permute-start | bytes 1597448 | tf_op jit(solution)/shard_map/ppermute | solution.py:28
  94.6 30.3 %collective-permute-start.28 = (f32[512,256]{1,0:T(8,128)S(1)}, f32[512,256]{1,0:T(8,128)S(1)}, u32[]{:S(2)}, u32[]{:S(2)}) collective-permute-start(f32[512,256]{1,0:T(8,128)S(1)} %pad_maximum_fusion.refs_10_.refs_11_), channel_id=1, source_target_pairs={{0,1},{1,0},{2,3},{3,2},{4,5},{5,4},{6,7},{7,6},{8,9},{9,8},{10,11... | collective-permute-start | bytes 1572872 | tf_op jit(solution)/shard_map/ppermute | solution.py:28
  107.2 15.0 %collective-permute-start.32 = (f32[520,256]{1,0:T(8,128)S(1)}, f32[520,256]{1,0:T(8,128)S(1)}, u32[]{:S(2)}, u32[]{:S(2)}) collective-permute-start(f32[520,256]{1,0:T(8,128)S(1)} %collective-permute-done.30.refs_8_), channel_id=1, source_target_pairs={{0,1},{1,0},{2,3},{3,2},{4,5},{5,4},{6,7},{7,6},{8,9},{9,8},{10,11... | collective-permute-start | bytes 1597448 | tf_op jit(solution)/shard_map/ppermute | solution.py:28
  107.2 15.0 %collective-permute-start.36 = (f32[520,256]{1,0:T(8,128)S(1)}, f32[520,256]{1,0:T(8,128)S(1)}, u32[]{:S(2)}, u32[]{:S(2)}) collective-permute-start(f32[520,256]{1,0:T(8,128)S(1)} %collective-permute-done.34.refs_16_), channel_id=1, source_target_pairs={{0,1},{1,0},{2,3},{3,2},{4,5},{5,4},{6,7},{7,6},{8,9},{9,8},{10,11... | collective-permute-start | bytes 1597448 | tf_op jit(solution)/shard_map/ppermute | solution.py:28
  118.2 7.4 %collective-permute-start.27 = (f32[520,256]{1,0:T(8,128)S(1)}, f32[520,256]{1,0:T(8,128)S(1)}, u32[]{:S(2)}, u32[]{:S(2)}) collective-permute-start(f32[520,256]{1,0:T(8,128)S(1)} %collective-permute-done.19.refs_9_), channel_id=1, source_target_pairs={{0,1},{1,0},{2,3},{3,2},{4,5},{5,4},{6,7},{7,6},{8,9},{9,8},{10,11... | collective-permute-start | bytes 1597448 | tf_op jit(solution)/shard_map/ppermute | solution.py:28
  121.9 3.7 %collective-permute-start.18 = (s32[8]{0:T(128)S(1)}, s32[8]{0:T(128)S(1)}, u32[]{:S(2)}, u32[]{:S(2)}) collective-permute-start(s32[8]{0:T(128)S(1)} %get-tuple-element.95.refs_1_), channel_id=1, source_target_pairs={{0,128},{1,129},{2,130},{3,131},{4,132},{5,133},{6,134},{7,135},{8... | collective-permute-start | bytes 104 | tf_op jit(solution)/shard_map/ppermute | solution.py:28
  129.1 35.4 %collective-permute-start.4 = (f32[5,256,256]{2,1,0:T(8,128)S(1)}, f32[5,256,256]{2,1,0:T(8,128)S(1)}, u32[]{:S(2)}, u32[]{:S(2)}) collective-permute-start(f32[5,256,256]{2,1,0:T(8,128)S(1)} %slice.56), channel_id=1, source_target_pairs={{0,128},{1,129},{2,130},{3,131},{4,132},{5,133},{6,134},{7,135},{8... | collective-permute-start | bytes 3932168 | tf_op jit(solution)/shard_map/cond/branch_4_fun/ppermute | solution.py:28
  165.6 1.3 copy-start.3

commit v2 on v1

--- a/solution.py
+++ b/solution.py
@@ -60,14 +60,16 @@
     return dot(a_high, b_high) + (dot(a_high, b_low) + dot(a_low, b_high))
 
 
-def scan_kernel(n_early, info, a_rows, a_cols, c_rows, c_cols, *refs):
-    notes, (told, *lists) = refs[:-5], refs[-5:]
-    for i in range(told.shape[0]):
+def scan_kernel(counts, first, before, info, a_rows, a_cols, c_rows, c_cols, *refs):
+    n_out = 1 + 2 * len(counts)
+    notes, (told, *lists) = refs[:-n_out], refs[-n_out:]
+    told[0] = before[0]
+    for i in range(1, told.shape[0]):
         told[i] = 0
-    for p in range(len(notes)):
-        group = info[p]
-        late = int(p >= n_early)
-        work, hits = lists[2 * late], lists[2 * late + 1]
+    places = [(part, i) for part, n in enumerate(counts) for i in range(n)]
+    for p, (part, inside) in enumerate(places):
+        group = info[first + p]
+        work, hits = lists[2 * part], lists[2 * part + 1]
 
         @pl.when(group >= 0)
         def _():
@@ -87,36 +89,37 @@
 
                         @pl.when(mask != 0)
                         def _():
-                            n = told[1 + late]
-                            work[n] = ((p - late * n_early) * A_SLOTS + m) * PANEL + q
+                            n = told[1 + part]
+                            work[n] = (inside * A_SLOTS + m) * PANEL + q
                             hits[n] = mask
-                            told[1 + late] = n + 1
+                            told[1 + part] = n + 1
                             told[0] = told[0] | mask
 
 
-def scan(info, tables, notes, n_early):
+def scan(counts, first, before, info, tables, notes):
     smem = pl.BlockSpec(memory_space=pltpu.SMEM)
-    sizes = [8] + 2 * [n_early * A_SLOTS * PANEL] + 2 * [(len(notes) - n_early) * A_SLOTS * PANEL]
+    sizes = [8] + [n * A_SLOTS * PANEL for n in counts for _ in range(2)]
     return pl.pallas_call(
-        functools.partial(scan_kernel, n_early),
+        functools.partial(scan_kernel, counts, first),
         out_shape=[jax.ShapeDtypeStruct((n,), jnp.int32) for n in sizes],
-        in_specs=[smem] * (5 + len(notes)),
-        out_specs=[smem] * 5,
+        in_specs=[smem] * (6 + len(notes)),
+        out_specs=[smem] * len(sizes),
         compiler_params=pltpu.CompilerParams(vmem_limit_bytes=2**20),
         name="scan",
-    )(info, *tables, *notes)
-
-
-def multiply_kernel(n_whole, n_split, last, info, told, work, hits, *refs):
+    )(before, info, *tables, *notes)
+
+
+def multiply_kernel(n_whole, n_split, base, part, first, last, info, told, work, hits, *refs):
     n_known = info.shape[0] // 2
-    base = n_known - n_split if last else 0
     if last:
         theirs, c_rows, c_cols, refs = *refs[:3], refs[3:]
     a_hbm, refs = refs[0], refs[1:]
     whole, refs = refs[:n_whole], refs[n_whole:]
     pieces, refs = refs[: 4 * n_split], refs[4 * n_split :]
+    if not first:
+        acc_in, refs = refs[0], refs[1:]
     if last:
-        acc_in, keep_out, send_out, plan, refs = *refs[:4], refs[4:]
+        keep_out, send_out, plan, refs = *refs[:3], refs[3:]
     else:
         acc_out, refs = refs[0], refs[1:]
     acc, a_buf, b_buf, sems, acc_sem = refs
@@ -124,12 +127,12 @@
     n_targets = acc.shape[0]
     half = n_targets // 2
 
-    if last:
+    if not first:
         load = pltpu.make_async_copy(acc_in, acc, acc_sem.at[0])
         load.start()
 
     per_panel = A_SLOTS * PANEL
-    total = told[1 + int(last)]
+    total = told[1 + part]
 
     def fetch_b(source, buf):
         pltpu.make_async_copy(source, b_buf.at[buf], sems.at[1, buf]).start()
@@ -165,10 +168,10 @@
     def _():
         fetch(0, 0)
 
-    if last:
+    if first:
+        acc[...] = jnp.zeros_like(acc)
+    else:
         load.wait()
-    else:
-        acc[...] = jnp.zeros_like(acc)
 
     @pl.loop(0, total)
     def _(n):
@@ -220,24 +223,24 @@
         out.wait()
 
 
-def multiply(info, found, theirs, a_blocks, whole, pieces, acc, n_targets):
+def multiply(info, found, base, part, theirs, a_blocks, whole, pieces, acc, n_targets):
     n_whole, n_split = len(whole), len(pieces) // 4
     size = a_blocks.shape[-1]
-    last = acc is not None
+    first, last = acc is None, theirs != []
     smem = pl.BlockSpec(memory_space=pltpu.SMEM)
     anywhere = pl.BlockSpec(memory_space=pl.ANY)
     full = jax.ShapeDtypeStruct((n_targets, size, size), jnp.float32)
-    part = jax.ShapeDtypeStruct((n_targets // 2, size, size), jnp.float32)
+    share = jax.ShapeDtypeStruct((n_targets // 2, size, size), jnp.float32)
     plan = jax.ShapeDtypeStruct((32,), jnp.int32)
     numbers = [info, *found, *theirs]
-    blocks = [a_blocks, *whole, *pieces] + ([acc] if last else [])
+    blocks = [a_blocks, *whole, *pieces] + ([] if first else [acc])
 
     def kernel(*refs):
-        multiply_kernel(n_whole, n_split, last, *refs)
+        multiply_kernel(n_whole, n_split, base, part, first, last, *refs)
 
     return pl.pallas_call(
         kernel,
-        out_shape=[part, part, plan] if last else full,
+        out_shape=[share, share, plan] if last else full,
         in_specs=[smem] * len(numbers) + [anywhere] * len(blocks),
         out_specs=[anywhere, anywhere, smem] if last else anywhere,
         scratch_shapes=[
@@ -323,22 +326,27 @@
     def of(part, i):
         return [x for stage in part for x in stage[i]]
 
-    early, late = stages[:REACH], stages[REACH:]
     info = jnp.stack(of(stages, 2) + of(stages, 3))
-    told, work0, hits0, work1, hits1 = scan(
-        info, tables, of(stages, 1), len(of(early, 1))
+    near, middle, far = stages[:2], stages[2:3], stages[3:]
+    found0 = scan([4], 0, jnp.zeros((8,), jnp.int32), info, tables, of(near, 1))
+    acc = multiply(
+        info, found0, 0, 0, [], a_blocks, [b_blocks, partner], of(near, 0), None, n_targets
+    )
+    told, work1, hits1, work2, hits2 = scan(
+        [2, 2], 4, found0[0], info, tables, of(middle, 1) + of(far, 1)
     )
     theirs = other_replica(told)
-    acc = multiply(
-        info, [told, work0, hits0], [], a_blocks, [b_blocks, partner], of(early, 0), None, n_targets
-    )
+    found1 = [told, work1, hits1]
+    acc = multiply(info, found1, 4, 0, [], a_blocks, [], of(middle, 0), acc, n_targets)
     keep, send, plan = multiply(
         info,
-        [told, work1, hits1],
+        [told, work2, hits2],
+        6,
+        1,
         [theirs, target_rows, target_cols],
         a_blocks,
         [],
-        of(late, 0),
+        of(far, 0),
         acc,
         n_targets,
     )

time: 167 us -> 179 us (1.072)
  waiting for transfers between devices: 96.7 us -> 106 us
  Pallas kernels: 10.4 us -> 12.6 us
    ppermute x31, waiting for transfers between devices: 96.7 us -> 106 us  [routed(): return lax.ppermute(value, BOTH, route)]
    pallas_call x3 -> x5, Pallas kernels: 9.33 us -> 11.6 us  [the longest x3 6.73 us: multiply(): pl.pallas_call(kernel, out_shape=[share, share, plan] if last else full,...]
  transfers between devices with their start and end apart: 31 -> 31, of which waited for: 12 -> 13; matrix products, arithmetic and copies ran while one was open for 3% -> 3% of each run, Pallas kernels for 4% -> 5%
where the time goes in v2:
time: 179 us
  waiting for transfers between devices  106 us (59%)
  starting transfers between devices  49 us (27%)
  Pallas kernels  12.6 us (7%)
  other arithmetic  5.93 us (3%)
  local copies, waits for them, and re-layouts  3.93 us (2%)
    ppermute x31, waiting for transfers between devices, routed(): return lax.ppermute(value, BOTH, route)  106 us
    ppermute x31, starting transfers between devices, routed(): return lax.ppermute(value, BOTH, route)  49 us
    pallas_call x3, Pallas kernels, multiply(): pl.pallas_call(kernel, out_shape=[share, share, plan] if last else full,...  6.73 us
    pallas_call x2, Pallas kernels, scan(): pl.pallas_call(functools.partial(scan_kernel, counts, first), out_shape=[...  4.84 us
  transfers between devices with their start and end apart: 31, of which 13 were waited for; matrix products, arithmetic and copies ran while one was open for 3% of the time, Pallas kernels for 5%

profile of v2, /device:TPU:2, one launch (start us, length us, event | category | flops | bytes accessed | tf_op | source)
XLA Modules:
  0.0 179.2 jit_solution(3992101766743523818)
XLA Ops:
  0.7 1.2 constant_dynamic-slice_fusion
  2.0 0.8 fusion.1
  2.7 0.8 select_maximum_fusion
  3.6 8.3 %collective-permute-start.10 = (f32[520,256]{1,0:T(8,128)}, f32[520,256]{1,0:T(8,128)S(1)}, u32[]{:S(2)}, u32[]{:S(2)}) collective-permute-start(f32[520,256]{1,0:T(8,128)} %select_maximum_fusion), channel_id=1, source_target_pairs={{0,254},{1,255},{2,0},{3,1},{4,2},{5,3},{6,4},{7,5},{8,6},{9,7},{1... | collective-permute-start | bytes 1597448 | tf_op jit(solution)/shard_map/ppermute | solution.py:28
  11.8 1.0 dynamic-slice_bitcast_fusion
  12.9 6.3 %collective-permute-start.23 = (f32[256,256]{1,0:T(8,128)S(1)}, f32[256,256]{1,0:T(8,128)}, u32[]{:S(2)}, u32[]{:S(2)}) collective-permute-start(f32[256,256]{1,0:T(8,128)S(1)} %dynamic-slice_bitcast_fusion), channel_id=1, source_target_pairs={{0,254},{1,255},{2,0},{3,1},{4,2},{5,3},{6,4},{7,5},{8,6},{9,7},{1... | collective-permute-start | bytes 786440 | tf_op jit(solution)/shard_map/ppermute | solution.py:28
  19.5 16.1 %collective-permute-done.20 = f32[256,256]{1,0:T(8,128)} collective-permute-done((f32[256,256]{1,0:T(8,128)S(1)}, f32[256,256]{1,0:T(8,128)}, u32[]{:S(2)}, u32[]{:S(2)}) %collective-permute-start.20) | collective-permute-done | bytes 262176 | tf_op jit(solution)/shard_map/ppermute | solution.py:28
  35.6 6.2 %collective-permute-start.24 = (f32[256,256]{1,0:T(8,128)}, f32[256,256]{1,0:T(8,128)}, u32[]{:S(2)}, u32[]{:S(2)}) collective-permute-start(f32[256,256]{1,0:T(8,128)} %collective-permute-done.23), channel_id=1, source_target_pairs={{0,254},{1,255},{2,0},{3,1},{4,2},{5,3},{6,4},{7,5},{8,6},{9,7},{1... | collective-permute-start | bytes 786440 | tf_op jit(solution)/shard_map/ppermute | solution.py:28
  41.8 1.8 broadcast_select_fusion.7
  43.8 0.1 stack.50.info.refs_0_
  43.9 3.1 %collective-permute-done.21 = f32[256,256]{1,0:T(8,128)} collective-permute-done((f32[256,256]{1,0:T(8,128)}, f32[256,256]{1,0:T(8,128)}, u32[]{:S(2)}, u32[]{:S(2)}) %collective-permute-start.21) | collective-permute-done | bytes 262176 | tf_op jit(solution)/shard_map/ppermute | solution.py:28
  47.1 1.1 broadcast_select_fusion.9
  48.2 2.1 %collective-permute-done.35 = f32[256,256]{1,0:T(8,128)} collective-permute-done((f32[256,256]{1,0:T(8,128)}, f32[256,256]{1,0:T(8,128)}, u32[]{:S(2)}, u32[]{:S(2)}) %collective-permute-start.35) | collective-permute-done | bytes 262176 | tf_op jit(solution)/shard_map/ppermute | solution.py:28
  50.3 4.2 %collective-permute-start.25 = (f32[256,256]{1,0:T(8,128)}, f32[256,256]{1,0:T(8,128)S(1)}, u32[]{:S(2)}, u32[]{:S(2)}) collective-permute-start(f32[256,256]{1,0:T(8,128)} %collective-permute-done.24), channel_id=1, source_target_pairs={{0,254},{1,255},{2,0},{3,1},{4,2},{5,3},{6,4},{7,5},{8,6},{9,7},{1... | collective-permute-start | bytes 786440 | tf_op jit(solution)/shard_map/ppermute | solution.py:28
  54.5 1.9 %collective-permute-start.13 = (f32[520,256]{1,0:T(8,128)S(1)}, f32[520,256]{1,0:T(8,128)S(1)}, u32[]{:S(2)}, u32[]{:S(2)}) collective-permute-start(f32[520,256]{1,0:T(8,128)S(1)} %collective-permute-done.10), channel_id=1, source_target_pairs={{0,254},{1,255},{2,0},{3,1},{4,2},{5,3},{6,4},{7,5},{8,6},{9,7},{1... | collective-permute-start | bytes 1597448 | tf_op jit(solution)/shard_map/ppermute | solution.py:28
  56.4 1.0 pad_maximum_fusion.2.refs_9_.refs_10_
  57.5 3.1 %collective-permute-done.22 = f32[256,256]{1,0:T(8,128)S(1)} collective-permute-done((f32[256,256]{1,0:T(8,128)}, f32[256,256]{1,0:T(8,128)S(1)}, u32[]{:S(2)}, u32[]{:S(2)}) %collective-permute-start.22) | collective-permute-done | bytes 262176 | tf_op jit(solution)/shard_map/ppermute | solution.py:28
  60.6 10.9 %collective-permute-done.12 = f32[520,256]{1,0:T(8,128)S(1)} collective-permute-done((f32[520,256]{1,0:T(8,128)S(1)}, f32[520,256]{1,0:T(8,128)S(1)}, u32[]{:S(2)}, u32[]{:S(2)}) %collective-permute-start.12) | collective-permute-done | bytes 532512 | tf_op jit(solution)/shard_map/ppermute | solution.py:28
  71.6 0.1 collective-permute-start.8
  71.7 0.4 collective-permute-done.13
  72.1 6.7 %collective-permute-start.16 = (f32[520,256]{1,0:T(8,128)S(1)}, f32[520,256]{1,0:T(8,128)S(1)}, u32[]{:S(2)}, u32[]{:S(2)}) collective-permute-start(f32[520,256]{1,0:T(8,128)S(1)} %collective-permute-done.13), channel_id=1, source_target_pairs={{0,254},{1,255},{2,0},{3,1},{4,2},{5,3},{6,4},{7,5},{8,6},{9,7},{1... | collective-permute-start | bytes 1597448 | tf_op jit(solution)/shard_map/ppermute | solution.py:28
  78.8 0.3 collective-permute-start.37
  79.2 0.6 collective-permute-start.11
  79.7 9.7 %collective-permute-done.15 = f32[520,256]{1,0:T(8,128)S(1)} collective-permute-done((f32[520,256]{1,0:T(8,128)S(1)}, f32[520,256]{1,0:T(8,128)S(1)}, u32[]{:S(2)}, u32[]{:S(2)}) %collective-permute-start.15) | collective-permute-done | bytes 532512 | tf_op jit(solution)/shard_map/ppermute | solution.py:28
  89.6 0.3 collective-permute-done.16
  89.9 1.8 %collective-permute-start.26 = (f32[256,256]{1,0:T(8,128)S(1)}, f32[256,256]{1,0:T(8,128)S(1)}, u32[]{:S(2)}, u32[]{:S(2)}) collective-permute-start(f32[256,256]{1,0:T(8,128)S(1)} %get-tuple-element.121), channel_id=1, source_target_pairs={{0,128},{1,129},{2,130},{3,131},{4,132},{5,133},{6,134},{7,135},{8... | collective-permute-start | bytes 786440 | tf_op jit(solution)/shard_map/ppermute | solution.py:28
  91.8 0.1 collective-permute-start.14
  91.9 16.0 %collective-permute-done.26 = f32[256,256]{1,0:T(8,128)S(1)} collective-permute-done((f32[256,256]{1,0:T(8,128)S(1)}, f32[256,256]{1,0:T(8,128)S(1)}, u32[]{:S(2)}, u32[]{:S(2)}) %collective-permute-start.26) | collective-permute-done | bytes 262176 | tf_op jit(solution)/shard_map/ppermute | solution.py:28
  107.9 0.3 collective-permute-start.29
  108.2 1.8 %collective-permute-start.19 = (f32[520,256]{1,0:T(8,128)S(1)}, f32[520,256]{1,0:T(8,128)S(1)}, u32[]{:S(2)}, u32[]{:S(2)}) collective-permute-start(f32[520,256]{1,0:T(8,128)S(1)} %get-tuple-element.114), channel_id=1, source_target_pairs={{0,128},{1,129},{2,130},{3,131},{4,132},{5,133},{6,134},{7,135},{8... | collective-permute-start | bytes 1597448 | tf_op jit(solution)/shard_map/ppermute | solution.py:28
  110.0 0.2 collective-permute-start.17
  110.3 1.9 %scan.2 = (s32[8]{0:T(128)S(1)}, s32[96]{0:T(128)S(1)}, s32[96]{0:T(128)S(1)}) custom-call(s32[8]{0:T(128)S(1)} %broadcast_3_before.2.before, s32[16]{0:T(128)S(1)} %stack.50.info.refs_0_, s32[24]{0:T(128)S(1)} %bitcast.72, s32[24]{0:T(128)S(1)} %bitcast.74, s32[16]{0:T(128)S(1)} %get-tuple-element.127.c_rows.refs_5_, ...), custom_call_target="tpu_custom_call" | custom-call | tf_op jit(solution)/shard_map/scan/pallas_call | solution.py:102
  112.2 1.0 collective-permute-start.32
  113.2 0.1 collective-permute-start.28
  113.3 9.5 %collective-permute-done.29.refs_6_ = f32[520,256]{1,0:T(8,128)S(1)} collective-permute-done((f32[520,256]{1,0:T(8,128)S(1)}, f32[520,256]{1,0:T(8,128)S(1)}, u32[]{:S(2)}, u32[]{:S(2)}) %collective-permute-start.29) | collective-permute-done | bytes 532512 | tf_op jit(solution)/shard_map/ppermute | solution.py:28
  122.8 8.4 %collective-permute-done.19.refs_9_ = f32[520,256]{1,0:T(8,128)S(1)} collective-permute-done((f32[520,256]{1,0:T(8,128)S(1)}, f32[520,256]{1,0:T(8,128)S(1)}, u32[]{:S(2)}, u32[]{:S(2)}) %collective-permute-start.19) | collective-permute-done | bytes 532512 | tf_op jit(solution)/shard_map/ppermute | solution.py:28
  131.2 2.5 %multiply.3.refs_13_ = f32[16,256,256]{2,1,0:T(8,128)S(1)} custom-call(s32[16]{0:T(128)S(1)} %stack.50.info.refs_0_, s32[8]{0:T(128)S(1)} %get-tuple-element.98.before.refs_1_, s32[96]{0:T(128)S(1)} %get-tuple-element.104.refs_2_, s32[96]{0:T(128)S(1)} %get-tuple-element.105.refs_3_, f32[24,256,256]{2,1,0:T(8,128)S(1)} %bitcast.65, ...), custom_call_target="tpu_custom_call" | custom-call | flops 268435456 | bytes 12582912 | tf_op jit(solution)/shard_map/multiply/pallas_call | solution.py:241
  133.8 2.9 %scan.3 = (s32[8]{0:T(128)S(1)}, s32[48]{0:T(128)S(1)}, s32[48]{0:T(128)S(1)}, s32[48]{0:T(128)S(1)}, s32[48]{0:T(128)S(1)}) custom-call(s32[8]{0:T(128)S(1)} %get-tuple-element.98.before.refs_1_, s32[16]{0:T(128)S(1)} %stack.50.info.refs_0_, s32[24]{0:T(128)S(1)} %bitcast.73, s32[24]{0:T(128)S(1)} %bitcast.75, s32[16]{0:T(128)S(1)} %get-tuple-element.127.c_rows.refs_5_, ...), custom_call_target="tpu_custom_call" | custom-call | tf_op jit(solution)/shard_map/scan/pallas_call | solution.py:102
  136.7 6.5 %collective-permute-start.18 = (s32[8]{0:T(128)S(1)}, s32[8]{0:T(128)S(1)}, u32[]{:S(2)}, u32[]{:S(2)}) collective-permute-start(s32[8]{0:T(128)S(1)} %get-tuple-element.99.refs_1_), channel_id=1, source_target_pairs={{0,128},{1,129},{2,130},{3,131},{4,132},{5,133},{6,134},{7,135},{8... | collective-permute-start | bytes 104 | tf_op jit(solution)/shard_map/ppermute | solution.py:28
  143.2 1.2 multiply.4.refs_16_
  144.4 0.3 collective-permute-done.18.refs_4_
  144.7 3.1 %multiply.5 = (f32[8,256,256]{2,1,0:T(8,128)S(1)}, f32[8,256,256]{2,1,0:T(8,128)S(1)}, s32[32]{0:T(128)S(1)}) custom-call(s32[16]{0:T(128)S(1)} %stack.50.info.refs_0_, s32[8]{0:T(128)S(1)} %get-tuple-element.99.refs_1_, s32[48]{0:T(128)S(1)} %get-tuple-element.100.refs_2_, s32[48]{0:T(128)S(1)} %get-tuple-element.101.refs_3_, ...), custom_call_target="tpu_custom_call" | custom-call | flops 268435456 | bytes 12582912 | tf_op jit(solution)/shard_map/multiply/pallas_call | solution.py:241
  147.8 30.0 %conditional.1 = (f32[1,8,256,256]{3,2,1,0:T(8,128)S(1)}) conditional(s32[]{:T(128)} %bitcast.41, (f32[8,256,256]{2,1,0:T(8,128)S(1)}, s32[32]{0:T(128)S(1)}, f32[8,256,256]{2,1,0:T(8,128)S(1)}) %tuple.37, (f32[8,256,256]{2,1,0:T(8,128)S(1)}, s32[32]{0:T(128)S(1)}, f32[8,256,256]{2,1,0:T(8,128)S(1)}) %tuple.37, ...), branch_computations={%region_0.1_spmd, %region_1.2_spmd, %region_2.3_spmd, %region_3.4_... | conditional | bytes 11010096 | solution.py:353
  148.1 0.1 slice.56
  148.2 2.4 %collective-permute-start.4 = (f32[5,256,256]{2,1,0:T(8,128)S(1)}, f32[5,256,256]{2,1,0:T(8,128)S(1)}, u32[]{:S(2)}, u32[]{:S(2)}) collective-permute-start(f32[5,256,256]{2,1,0:T(8,128)S(1)} %slice.56), channel_id=1, source_target_pairs={{0,128},{1,129},{2,130},{3,131},{4,132},{5,133},{6,134},{7,135},{8... | collective-permute-start | bytes 3932168 | tf_op jit(solution)/shard_map/cond/branch_4_fun/ppermute | solution.py:28
  150.6 26.2 %collective-permute-done.4.come = f32[5,256,256]{2,1,0:T(8,128)S(1)} collective-permute-done((f32[5,256,256]{2,1,0:T(8,128)S(1)}, f32[5,256,256]{2,1,0:T(8,128)S(1)}, u32[]{:S(2)}, u32[]{:S(2)}) %collective-permute-start.4) | collective-permute-done | bytes 1310752 | tf_op jit(solution)/shard_map/cond/branch_4_fun/ppermute | solution.py:28
  176.8 1.0 finish.12
  177.9 1.3 copy-done.3
  (70 shorter events, 1.0 us)
Async XLA Ops:
  0.0 43.6 %copy-start.7 = (s32[1,6]{1,0:T(1,128)S(1)}, s32[1,6]{1,0:T(1,128)}, u32[]{:S(2)}) copy-start(s32[1,6]{1,0:T(1,128)} %param.21) | copy-start | bytes 76
  0.0 43.6 %copy-start.6 = (s32[1,6]{1,0:T(1,128)S(1)}, s32[1,6]{1,0:T(1,128)}, u32[]{:S(2)}) copy-start(s32[1,6]{1,0:T(1,128)} %param.22) | copy-start | bytes 76
  0.0 19.2 %copy-start.4 = (s32[1,16]{1,0:T(1,128)S(1)}, s32[1,16]{1,0:T(1,128)}, u32[]{:S(2)}) copy-start(s32[1,16]{1,0:T(1,128)} %param.25) | copy-start | bytes 196
  0.0 19.3 %copy-start.5 = (s32[1,16]{1,0:T(1,128)S(1)}, s32[1,16]{1,0:T(1,128)}, u32[]{:S(2)}) copy-start(s32[1,16]{1,0:T(1,128)} %param.24) | copy-start | bytes 196
  0.7 130.5 %slice-start = ((s8[6291456]{0:T(1024)(128)(4,1)}), s8[2097152]{0:T(1024)(128)(4,1)S(1)}, s32[]{:S(2)}) async-start(s8[6291456]{0:T(1024)(128)(4,1)} %bitcast.63), calls=%async_computation | async-start | bytes 4194304
  3.6 50.9 %collective-permute-start.10 = (f32[520,256]{1,0:T(8,128)}, f32[520,256]{1,0:T(8,128)S(1)}, u32[]{:S(2)}, u32[]{:S(2)}) collective-permute-start(f32[520,256]{1,0:T(8,128)} %select_maximum_fusion), channel_id=1, source_target_pairs={{0,254},{1,255},{2,0},{3,1},{4,2},{5,3},{6,4},{7,5},{8,6},{9,7},{1... | collective-permute-start | bytes 1597448 | tf_op jit(solution)/shard_map/ppermute | solution.py:28
  11.8 35.2 %collective-permute-start.9 = (f32[520,256]{1,0:T(8,128)}, f32[520,256]{1,0:T(8,128)S(1)}, u32[]{:S(2)}, u32[]{:S(2)}) collective-permute-start(f32[520,256]{1,0:T(8,128)} %select_maximum_fusion), channel_id=1, source_target_pairs={{0,2},{1,3},{2,4},{3,5},{4,6},{5,7},{6,8},{7,9},{8,10},{9,11},{10,... | collective-permute-start | bytes 1597448 | tf_op jit(solution)/shard_map/ppermute | solution.py:28
  12.8 22.7 %collective-permute-start.20 = (f32[256,256]{1,0:T(8,128)S(1)}, f32[256,256]{1,0:T(8,128)}, u32[]{:S(2)}, u32[]{:S(2)}) collective-permute-start(f32[256,256]{1,0:T(8,128)S(1)} %dynamic-slice_bitcast_fusion), channel_id=1, source_target_pairs={{0,2},{1,3},{2,4},{3,5},{4,6},{5,7},{6,8},{7,9},{8,10},{9,11},{10,... | collective-permute-start | bytes 786440 | tf_op jit(solution)/shard_map/ppermute | solution.py:28
  12.9 22.7 %collective-permute-start.23 = (f32[256,256]{1,0:T(8,128)S(1)}, f32[256,256]{1,0:T(8,128)}, u32[]{:S(2)}, u32[]{:S(2)}) collective-permute-start(f32[256,256]{1,0:T(8,128)S(1)} %dynamic-slice_bitcast_fusion), channel_id=1, source_target_pairs={{0,254},{1,255},{2,0},{3,1},{4,2},{5,3},{6,4},{7,5},{8,6},{9,7},{1... | collective-permute-start | bytes 786440 | tf_op jit(solution)/shard_map/ppermute | solution.py:28
  35.6 11.4 %collective-permute-start.21 = (f32[256,256]{1,0:T(8,128)}, f32[256,256]{1,0:T(8,128)}, u32[]{:S(2)}, u32[]{:S(2)}) collective-permute-start(f32[256,256]{1,0:T(8,128)} %collective-permute-done.20), channel_id=1, source_target_pairs={{0,2},{1,3},{2,4},{3,5},{4,6},{5,7},{6,8},{7,9},{8,10},{9,11},{10,... | collective-permute-start | bytes 786440 | tf_op jit(solution)/shard_map/ppermute | solution.py:28
  35.6 11.4 %collective-permute-start.24 = (f32[256,256]{1,0:T(8,128)}, f32[256,256]{1,0:T(8,128)}, u32[]{:S(2)}, u32[]{:S(2)}) collective-permute-start(f32[256,256]{1,0:T(8,128)} %collective-permute-done.23), channel_id=1, source_target_pairs={{0,254},{1,255},{2,0},{3,1},{4,2},{5,3},{6,4},{7,5},{8,6},{9,7},{1... | collective-permute-start | bytes 786440 | tf_op jit(solution)/shard_map/ppermute | solution.py:28
  43.6 6.7 %collective-permute-start.35 = (f32[256,256]{1,0:T(8,128)}, f32[256,256]{1,0:T(8,128)}, u32[]{:S(2)}, u32[]{:S(2)}) collective-permute-start(f32[256,256]{1,0:T(8,128)} %get-tuple-element.117), channel_id=1, source_target_pairs={{0,128},{1,129},{2,130},{3,131},{4,132},{5,133},{6,134},{7,135},{8... | collective-permute-start | bytes 786440 | tf_op jit(solution)/shard_map/ppermute | solution.py:28
  47.0 63.0 %collective-permute-start.33 = (f32[6,256,256]{2,1,0:T(8,128)}, f32[6,256,256]{2,1,0:T(8,128)S(1)}, u32[]{:S(2)}, u32[]{:S(2)}) collective-permute-start(f32[6,256,256]{2,1,0:T(8,128)} %bitcast.70), channel_id=1, source_target_pairs={{0,1},{1,0},{2,3},{3,2},{4,5},{5,4},{6,7},{7,6},{8,9},{9,8},{10,11... | collective-permute-start | bytes 4718600 | tf_op jit(solution)/shard_map/ppermute | solution.py:28
  47.0 13.6 %collective-permute-start.22 = (f32[256,256]{1,0:T(8,128)}, f32[256,256]{1,0:T(8,128)S(1)}, u32[]{:S(2)}, u32[]{:S(2)}) collective-permute-start(f32[256,256]{1,0:T(8,128)} %collective-permute-done.21), channel_id=1, source_target_pairs={{0,2},{1,3},{2,4},{3,5},{4,6},{5,7},{6,8},{7,9},{8,10},{9,11},{10,... | collective-permute-start | bytes 786440 | tf_op jit(solution)/shard_map/ppermute | solution.py:28
  47.0 24.5 %collective-permute-start.12 = (f32[520,256]{1,0:T(8,128)S(1)}, f32[520,256]{1,0:T(8,128)S(1)}, u32[]{:S(2)}, u32[]{:S(2)}) collective-permute-start(f32[520,256]{1,0:T(8,128)S(1)} %collective-permute-done.9), channel_id=1, source_target_pairs={{0,2},{1,3},{2,4},{3,5},{4,6},{5,7},{6,8},{7,9},{8,10},{9,11},{10,... | collective-permute-start | bytes 1597448 | tf_op jit(solution)/shard_map/ppermute | solution.py:28
  50.3 21.3 %collective-permute-start.25 = (f32[256,256]{1,0:T(8,128)}, f32[256,256]{1,0:T(8,128)S(1)}, u32[]{:S(2)}, u32[]{:S(2)}) collective-permute-start(f32[256,256]{1,0:T(8,128)} %collective-permute-done.24), channel_id=1, source_target_pairs={{0,254},{1,255},{2,0},{3,1},{4,2},{5,3},{6,4},{7,5},{8,6},{9,7},{1... | collective-permute-start | bytes 786440 | tf_op jit(solution)/shard_map/ppermute | solution.py:28
  54.5 17.6 %collective-permute-start.13 = (f32[520,256]{1,0:T(8,128)S(1)}, f32[520,256]{1,0:T(8,128)S(1)}, u32[]{:S(2)}, u32[]{:S(2)}) collective-permute-start(f32[520,256]{1,0:T(8,128)S(1)} %collective-permute-done.10), channel_id=1, source_target_pairs={{0,254},{1,255},{2,0},{3,1},{4,2},{5,3},{6,4},{7,5},{8,6},{9,7},{1... | collective-permute-start | bytes 1597448 | tf_op jit(solution)/shard_map/ppermute | solution.py:28
  57.4 73.8 %slice-start.1 = ((s8[6291456]{0:T(1024)(128)(4,1)}), s8[4194304]{0:T(1024)(128)(4,1)S(1)}, s32[]{:S(2)}) async-start(s8[6291456]{0:T(1024)(128)(4,1)} %bitcast.63), calls=%async_computation.1 | async-start | bytes 8388608
  60.6 18.2 %collective-permute-start.30 = (f32[256,256]{1,0:T(8,128)S(1)}, f32[256,256]{1,0:T(8,128)S(1)}, u32[]{:S(2)}, u32[]{:S(2)}) collective-permute-start(f32[256,256]{1,0:T(8,128)S(1)} %get-tuple-element.119), channel_id=1, source_target_pairs={{0,128},{1,129},{2,130},{3,131},{4,132},{5,133},{6,134},{7,135},{8... | collective-permute-start | bytes 786440 | tf_op jit(solution)/shard_map/ppermute | solution.py:28
  71.6 17.9 %collective-permute-start.15 = (f32[520,256]{1,0:T(8,128)S(1)}, f32[520,256]{1,0:T(8,128)S(1)}, u32[]{:S(2)}, u32[]{:S(2)}) collective-permute-start(f32[520,256]{1,0:T(8,128)S(1)} %collective-permute-done.12), channel_id=1, source_target_pairs={{0,2},{1,3},{2,4},{3,5},{4,6},{5,7},{6,8},{7,9},{8,10},{9,11},{10,... | collective-permute-start | bytes 1597448 | tf_op jit(solution)/shard_map/ppermute | solution.py:28
  71.6 7.6 %collective-permute-start.8 = (s32[16]{0:T(128)S(1)}, s32[16]{0:T(128)S(1)}, u32[]{:S(2)}, u32[]{:S(2)}) collective-permute-start(s32[16]{0:T(128)S(1)} %pad_add_fusion.refs_0_), channel_id=1, source_target_pairs={{0,1},{1,0},{2,3},{3,2},{4,5},{5,4},{6,7},{7,6},{8,9},{9,8},{10,11... | collective-permute-start | bytes 200 | tf_op jit(solution)/shard_map/ppermute | solution.py:28
  72.1 17.8 %collective-permute-start.16 = (f32[520,256]{1,0:T(8,128)S(1)}, f32[520,256]{1,0:T(8,128)S(1)}, u32[]{:S(2)}, u32[]{:S(2)}) collective-permute-start(f32[520,256]{1,0:T(8,128)S(1)} %collective-permute-done.13), channel_id=1, source_target_pairs={{0,254},{1,255},{2,0},{3,1},{4,2},{5,3},{6,4},{7,5},{8,6},{9,7},{1... | collective-permute-start | bytes 1597448 | tf_op jit(solution)/shard_map/ppermute | solution.py:28
  78.8 12.9 %collective-permute-start.37 = (f32[512,256]{1,0:T(8,128)S(1)}, f32[512,256]{1,0:T(8,128)S(1)}, u32[]{:S(2)}, u32[]{:S(2)}) collective-permute-start(f32[512,256]{1,0:T(8,128)S(1)} %pad_maximum_fusion.2.refs_9_.refs_10_), channel_id=1, source_target_pairs={{0,1},{1,0},{2,3},{3,2},{4,5},{5,4},{6,7},{7,6},{8,9},{9,8},{10,11... | collective-permute-start | bytes 1572872 | tf_op jit(solution)/shard_map/ppermute | solution.py:28
  79.2 29.0 %collective-permute-start.11 = (f32[520,256]{1,0:T(8,128)S(1)}, f32[520,256]{1,0:T(8,128)S(1)}, u32[]{:S(2)}, u32[]{:S(2)}) collective-permute-start(f32[520,256]{1,0:T(8,128)S(1)} %get-tuple-element.111.refs_7_), channel_id=1, source_target_pairs={{0,1},{1,0},{2,3},{3,2},{4,5},{5,4},{6,7},{7,6},{8,9},{9,8},{10,11... | collective-permute-start | bytes 1597448 | tf_op jit(solution)/shard_map/ppermute | solution.py:28
  89.4 18.7 %collective-permute-start.34 = (f32[520,256]{1,0:T(8,128)S(1)}, f32[520,256]{1,0:T(8,128)S(1)}, u32[]{:S(2)}, u32[]{:S(2)}) collective-permute-start(f32[520,256]{1,0:T(8,128)S(1)} %get-tuple-element.110), channel_id=1, source_target_pairs={{0,128},{1,129},{2,130},{3,131},{4,132},{5,133},{6,134},{7,135},{8... | collective-permute-start | bytes 1597448 | tf_op jit(solution)/shard_map/ppermute | solution.py:28
  89.5 20.8 %copy-start.1 = (s32[1,24]{1,0:T(1,128)S(1)}, s32[1,24]{1,0:T(1,128)}, u32[]{:S(2)}) copy-start(s32[1,24]{1,0:T(1,128)} %param.18) | copy-start | bytes 292
  89.5 20.7 %copy-start.2 = (s32[1,24]{1,0:T(1,128)S(1)}, s32[1,24]{1,0:T(1,128)}, u32[]{:S(2)}) copy-start(s32[1,24]{1,0:T(1,128)} %param.19) | copy-start | bytes 292
  89.5 41.7 %copy-start = (f32[1,6,256,256]{3,2,1,0:T(8,128)S(1)}, f32[1,6,256,256]{3,2,1,0:T(8,128)}, u32[]{:S(2)}) copy-start(f32[1,6,256,256]{3,2,1,0:T(8,128)} %param.20) | copy-start | bytes 4718596
  89.9 18.0 %collective-permute-start.26 = (f32[256,256]{1,0:T(8,128)S(1)}, f32[256,256]{1,0:T(8,128)S(1)}, u32[]{:S(2)}, u32[]{:S(2)}) collective-permute-start(f32[256,256]{1,0:T(8,128)S(1)} %get-tuple-element.121), channel_id=1, source_target_pairs={{0,128},{1,129},{2,130},{3,131},{4,132},{5,133},{6,134},{7,135},{8... | collective-permute-start | bytes 786440 | tf_op jit(solution)/shard_map/ppermute | solution.py:28
  91.8 21.4 %collective-permute-start.14 = (f32[520,256]{1,0:T(8,128)S(1)}, f32[520,256]{1,0:T(8,128)S(1)}, u32[]{:S(2)}, u32[]{:S(2)}) collective-permute-start(f32[520,256]{1,0:T(8,128)S(1)} %get-tuple-element.113.refs_5_), channel_id=1, source_target_pairs={{0,1},{1,0},{2,3},{3,2},{4,5},{5,4},{6,7},{7,6},{8,9},{9,8},{10,11... | collective-permute-start | bytes 1597448 | tf_op jit(solution)/shard_map/ppermute | solution.py:28
  107.9 15.0 %collective-permute-start.29 = (f32[520,256]{1,0:T(8,128)S(1)}, f32[520,256]{1,0:T(8,128)S(1)}, u32[]{:S(2)}, u32[]{:S(2)}) collective-permute-start(f32[520,256]{1,0:T(8,128)S(1)} %get-tuple-element.112), channel_id=1, source_target_pairs={{0,128},{1,129},{2,130},{3,131},{4,132},{5,133},{6,134},{7,135},{8... | collective-permute-start | bytes 1597448 | tf_op jit(solution)/shard_map/ppermute | solution.py:28
  108.1 4.1 %collective-permute-start.36 = (f32[520,256]{1,0:T(8,128)S(1)}, f32[520,256]{1,0:T(8,128)S(1)}, u32[]{:S(2)}, u32[]{:S(2)}) collective-permute-start(f32[520,256]{1,0:T(8,128)S(1)} %collective-permute-done.34.refs_8_), channel_id=1, source_target_pairs={{0,1},{1,0},{2,3},{3,2},{4,5},{5,4},{6,7},{7,6},{8,9},{9,8},{10,11... | collective-permute-start | bytes 1597448 | tf_op jit(solution)/shard_map/ppermute | solution.py:28
  108.2 23.1 %collective-permute-start.19 = (f32[520,256]{1,0:T(8,128)S(1)}, f32[520,256]{1,0:T(8,128)S(1)}, u32[]{:S(2)}, u32[]{:S(2)}) collective-permute-start(f32[520,256]{1,0:T(8,128)S(1)} %get-tuple-element.114), channel_id=1, source_target_pairs={{0,128},{1,129},{2,130},{3,131},{4,132},{5,133},{6,134},{7,135},{8... | collective-permute-start | bytes 1597448 | tf_op jit(solution)/shard_map/ppermute | solution.py:28
  110.0 23.7 %collective-permute-start.17 = (f32[520,256]{1,0:T(8,128)S(1)}, f32[520,256]{1,0:T(8,128)S(1)}, u32[]{:S(2)}, u32[]{:S(2)}) collective-permute-start(f32[520,256]{1,0:T(8,128)S(1)} %get-tuple-element.115.refs_8_), channel_id=1, source_target_pairs={{0,1},{1,0},{2,3},{3,2},{4,5},{5,4},{6,7},{7,6},{8,9},{9,8},{10,11... | collective-permute-start | bytes 1597448 | tf_op jit(solution)/shard_map/ppermute | solution.py:28
  112.2 30.9 %collective-permute-start.32 = (f32[512,256]{1,0:T(8,128)S(1)}, f32[512,256]{1,0:T(8,128)S(1)}, u32[]{:S(2)}, u32[]{:S(2)}) collective-permute-start(f32[512,256]{1,0:T(8,128)S(1)} %pad_maximum_fusion.1.refs_7_.refs_8_), channel_id=1, source_target_pairs={{0,1},{1,0},{2,3},{3,2},{4,5},{5,4},{6,7},{7,6},{8,9},{9,8},{10,11... | collective-permute-start | bytes 1572872 | tf_op jit(solution)/shard_map/ppermute | solution.py:28
  113.2 31.2 %collective-permute-start.28 = (f32[512,256]{1,0:T(8,128)S(1)}, f32[512,256]{1,0:T(8,128)S(1)}, u32[]{:S(2)}, u32[]{:S(2)}) collective-permute-start(f32[512,256]{1,0:T(8,128)S(1)} %pad_maximum_fusion.refs_10_.refs_11_), channel_id=1, source_target_pairs={{0,1},{1,0},{2,3},{3,2},{4,5},{5,4},{6,7},{7,6},{8,9},{9,8},{10,11... | collective-permute-start | bytes 1572872 | tf_op jit(solution)/shard_map/ppermute | solution.py:28
  122.8 20.3 %collective-permute-start.31 = (f32[520,256]{1,0:T(8,128)S(1)}, f32[520,256]{1,0:T(8,128)S(1)}, u32[]{:S(2)}, u32[]{:S(2)}) collective-permute-start(f32[520,256]{1,0:T(8,128)S(1)} %collective-permute-done.29.refs_6_), channel_id=1, source_target_pairs={{0,1},{1,0},{2,3},{3,2},{4,5},{5,4},{6,7},{7,6},{8,9},{9,8},{10,11... | collective-permute-start | bytes 1597448 | tf_op jit(solution)/shard_map/ppermute | solution.py:28
  131.2 13.5 %collective-permute-start.27 = (f32[520,256]{1,0:T(8,128)S(1)}, f32[520,256]{1,0:T(8,128)S(1)}, u32[]{:S(2)}, u32[]{:S(2)}) collective-permute-start(f32[520,256]{1,0:T(8,128)S(1)} %collective-permute-done.19.refs_9_), channel_id=1, source_target_pairs={{0,1},{1,0},{2,3},{3,2},{4,5},{5,4},{6,7},{7,6},{8,9},{9,8},{10,11... | collective-permute-start | bytes 1597448 | tf_op jit(solution)/shard_map/ppermute | solution.py:28
  136.7 8.0 %collective-permute-start.18 = (s32[8]{0:T(128)S(1)}, s32[8]{0:T(128)S(1)}, u32[]{:S(2)}, u32[]{:S(2)}) collective-permute-start(s32[8]{0:T(128)S(1)} %get-tuple-element.99.refs_1_), channel_id=1, source_target_pairs={{0,128},{1,129},{2,130},{3,131},{4,132},{5,133},{6,134},{7,135},{8... | collective-permute-start | bytes 104 | tf_op jit(solution)/shard_map/ppermute | solution.py:28
  148.2 28.6 %collective-permute-start.4 = (f32[5,256,256]{2,1,0:T(8,128)S(1)}, f32[5,256,256]{2,1,0:T(8,128)S(1)}, u32[]{:S(2)}, u32[]{:S(2)}) collective-permute-start(f32[5,256,256]{2,1,0:T(8,128)S(1)} %slice.56), channel_id=1, source_target_pairs={{0,128},{1,129},{2,130},{3,131},{4,132},{5,133},{6,134},{7,135},{8... | collective-permute-start | bytes 3932168 | tf_op jit(solution)/shard_map/cond/branch_4_fun/ppermute | solution.py:28
  177.9 1.3 copy-start.3

commit v3 on v1

--- a/solution.py
+++ b/solution.py
@@ -13,6 +13,7 @@
 PANEL = 6
 HALF = 3
 FRONT = 2
+STRIDE = 1024
 RUN = 8
 REACH = 3
 BOTH = ("rep", "blk")
@@ -80,15 +81,17 @@
                     @pl.when(a_cols[slot] == notes[p][q])
                     def _():
                         row, col = a_rows[slot], notes[p][PANEL + q]
-                        mask = jnp.int32(0)
+                        mask, head = jnp.int32(0), jnp.int32(0)
                         for t in range(c_rows.shape[0]):
                             hit = (c_rows[t] == row) & (c_cols[t] == col)
                             mask = mask + jnp.where(hit, 1 << t, 0)
+                            head = jnp.where(hit, t, head)
 
                         @pl.when(mask != 0)
                         def _():
                             n = told[1 + late]
-                            work[n] = ((p - late * n_early) * A_SLOTS + m) * PANEL + q
+                            place = ((p - late * n_early) * A_SLOTS + m) * PANEL + q
+                            work[n] = head * STRIDE + place
                             hits[n] = mask
                             told[1 + late] = n + 1
                             told[0] = told[0] | mask
@@ -135,7 +138,7 @@
         pltpu.make_async_copy(source, b_buf.at[buf], sems.at[1, buf]).start()
 
     def fetch(n, buf):
-        i = work[n]
+        i = lax.rem(work[n], STRIDE)
         panel = lax.div(i, per_panel)
         rest = lax.rem(i, per_panel)
         a_slot = info[base + panel] * A_SLOTS + lax.div(rest, PANEL)
@@ -181,13 +184,16 @@
         pltpu.make_async_copy(a_hbm.at[0], a_buf.at[buf], sems.at[0, buf]).wait()
         pltpu.make_async_copy(a_hbm.at[0], b_buf.at[buf], sems.at[1, buf]).wait()
         term = product(a_buf[buf], b_buf[buf])
-        mask = hits[n]
-
-        @pl.loop(0, n_targets)
-        def _(t):
-            @pl.when(lax.rem(lax.shift_right_logical(mask, t), 2) == 1)
-            def _():
-                acc[t] = acc[t] + term
+        head = lax.div(work[n], STRIDE)
+        acc[head] = acc[head] + term
+
+        @pl.when(hits[n] != lax.shift_left(jnp.int32(1), head))
+        def _():
+            @pl.loop(0, n_targets)
+            def _(t):
+                @pl.when((t != head) & (lax.rem(lax.shift_right_logical(hits[n], t), 2) == 1))
+                def _():
+                    acc[t] = acc[t] + term
 
     if last:
         kept = pltpu.make_async_copy(acc.at[pl.ds(0, half)], keep_out, acc_sem.at[1])

time: 167 us -> 164 us (0.982)
  starting transfers between devices: 48.4 us -> 44.7 us
    ppermute x31, starting transfers between devices: 48.4 us -> 44.7 us  [routed(): return lax.ppermute(value, BOTH, route)]
where the time goes in v3:
time: 164 us
  waiting for transfers between devices  98.2 us (60%)
  starting transfers between devices  44.7 us (27%)
  Pallas kernels  9.65 us (6%)
  other arithmetic  6.05 us (4%)
  local copies, waits for them, and re-layouts  3.93 us (2%)
    ppermute x31, waiting for transfers between devices, routed(): return lax.ppermute(value, BOTH, route)  98.2 us
    ppermute x31, starting transfers between devices, routed(): return lax.ppermute(value, BOTH, route)  44.7 us
    pallas_call x2, Pallas kernels, multiply(): pl.pallas_call(kernel, out_shape=[part, part, plan] if last else full, in...  4.73 us
    pallas_call x1, Pallas kernels, scan(): pl.pallas_call(functools.partial(scan_kernel, n_early), out_shape=[jax.Sh...  3.87 us
  transfers between devices with their start and end apart: 31, of which 12 were waited for; matrix products, arithmetic and copies ran while one was open for 3% of the time, Pallas kernels for 4%

profile of v3, /device:TPU:2, one launch (start us, length us, event | category | flops | bytes accessed | tf_op | source)
XLA Modules:
  0.0 164.0 jit_solution(1767484868155262226)
XLA Ops:
  0.7 1.2 constant_dynamic-slice_fusion
  2.0 0.8 fusion.1
  2.7 0.8 select_maximum_fusion
  3.6 1.9 %collective-permute-start.9 = (f32[520,256]{1,0:T(8,128)}, f32[520,256]{1,0:T(8,128)S(1)}, u32[]{:S(2)}, u32[]{:S(2)}) collective-permute-start(f32[520,256]{1,0:T(8,128)} %select_maximum_fusion), channel_id=1, source_target_pairs={{0,2},{1,3},{2,4},{3,5},{4,6},{5,7},{6,8},{7,9},{8,10},{9,11},{10,... | collective-permute-start | bytes 1597448 | tf_op jit(solution)/shard_map/ppermute | solution.py:29
  5.5 6.4 %collective-permute-start.10 = (f32[520,256]{1,0:T(8,128)}, f32[520,256]{1,0:T(8,128)S(1)}, u32[]{:S(2)}, u32[]{:S(2)}) collective-permute-start(f32[520,256]{1,0:T(8,128)} %select_maximum_fusion), channel_id=1, source_target_pairs={{0,254},{1,255},{2,0},{3,1},{4,2},{5,3},{6,4},{7,5},{8,6},{9,7},{1... | collective-permute-start | bytes 1597448 | tf_op jit(solution)/shard_map/ppermute | solution.py:29
  11.8 1.0 dynamic-slice_bitcast_fusion
  12.8 0.1 collective-permute-start.20
  12.9 6.2 %collective-permute-start.23 = (f32[256,256]{1,0:T(8,128)S(1)}, f32[256,256]{1,0:T(8,128)}, u32[]{:S(2)}, u32[]{:S(2)}) collective-permute-start(f32[256,256]{1,0:T(8,128)S(1)} %dynamic-slice_bitcast_fusion), channel_id=1, source_target_pairs={{0,254},{1,255},{2,0},{3,1},{4,2},{5,3},{6,4},{7,5},{8,6},{9,7},{1... | collective-permute-start | bytes 786440 | tf_op jit(solution)/shard_map/ppermute | solution.py:29
  19.4 10.5 %collective-permute-done.20 = f32[256,256]{1,0:T(8,128)} collective-permute-done((f32[256,256]{1,0:T(8,128)S(1)}, f32[256,256]{1,0:T(8,128)}, u32[]{:S(2)}, u32[]{:S(2)}) %collective-permute-start.20) | collective-permute-done | bytes 262176 | tf_op jit(solution)/shard_map/ppermute | solution.py:29
  29.9 6.2 %collective-permute-start.24 = (f32[256,256]{1,0:T(8,128)}, f32[256,256]{1,0:T(8,128)}, u32[]{:S(2)}, u32[]{:S(2)}) collective-permute-start(f32[256,256]{1,0:T(8,128)} %collective-permute-done.23), channel_id=1, source_target_pairs={{0,254},{1,255},{2,0},{3,1},{4,2},{5,3},{6,4},{7,5},{8,6},{9,7},{1... | collective-permute-start | bytes 786440 | tf_op jit(solution)/shard_map/ppermute | solution.py:29
  36.1 1.8 %broadcast_select_fusion.9 = (f32[256,256]{1,0:T(8,128)S(1)}, f32[256,256]{1,0:T(8,128)}) fusion(f32[256,256]{1,0:T(8,128)} %collective-permute-done.20, f32[256,256]{1,0:T(8,128)} %collective-permute-done.23, pred[]{:T(512)S(6)} %eq.6), kind=kLoop, calls=%fused_computation.15 | loop fusion | flops 131072 | bytes 1048577 | tf_op jit(solution)/shard_map/jit(_where)/select_n | solution.py:317
  38.1 0.1 stack.50.info.refs_0_
  38.2 0.1 collective-permute-start.12
  38.3 3.6 %collective-permute-done.21 = f32[256,256]{1,0:T(8,128)} collective-permute-done((f32[256,256]{1,0:T(8,128)}, f32[256,256]{1,0:T(8,128)}, u32[]{:S(2)}, u32[]{:S(2)}) %collective-permute-start.21) | collective-permute-done | bytes 262176 | tf_op jit(solution)/shard_map/ppermute | solution.py:29
  41.9 1.1 broadcast_select_fusion.7
  43.0 0.1 collective-permute-start.35
  43.1 0.1 collective-permute-start.22
  43.1 3.0 %collective-permute-done.31 = f32[256,256]{1,0:T(8,128)} collective-permute-done((f32[256,256]{1,0:T(8,128)}, f32[256,256]{1,0:T(8,128)}, u32[]{:S(2)}, u32[]{:S(2)}) %collective-permute-start.31) | collective-permute-done | bytes 262176 | tf_op jit(solution)/shard_map/ppermute | solution.py:29
  46.1 3.2 %collective-permute-start.25 = (f32[256,256]{1,0:T(8,128)}, f32[256,256]{1,0:T(8,128)S(1)}, u32[]{:S(2)}, u32[]{:S(2)}) collective-permute-start(f32[256,256]{1,0:T(8,128)} %collective-permute-done.24), channel_id=1, source_target_pairs={{0,254},{1,255},{2,0},{3,1},{4,2},{5,3},{6,4},{7,5},{8,6},{9,7},{1... | collective-permute-start | bytes 786440 | tf_op jit(solution)/shard_map/ppermute | solution.py:29
  49.4 1.7 %collective-permute-start.13 = (f32[520,256]{1,0:T(8,128)S(1)}, f32[520,256]{1,0:T(8,128)S(1)}, u32[]{:S(2)}, u32[]{:S(2)}) collective-permute-start(f32[520,256]{1,0:T(8,128)S(1)} %collective-permute-done.10), channel_id=1, source_target_pairs={{0,254},{1,255},{2,0},{3,1},{4,2},{5,3},{6,4},{7,5},{8,6},{9,7},{1... | collective-permute-start | bytes 1597448 | tf_op jit(solution)/shard_map/ppermute | solution.py:29
  51.1 1.1 pad_maximum_fusion.1.refs_9_.refs_10_
  52.3 8.5 %collective-permute-done.22 = f32[256,256]{1,0:T(8,128)S(1)} collective-permute-done((f32[256,256]{1,0:T(8,128)}, f32[256,256]{1,0:T(8,128)S(1)}, u32[]{:S(2)}, u32[]{:S(2)}) %collective-permute-start.22) | collective-permute-done | bytes 262176 | tf_op jit(solution)/shard_map/ppermute | solution.py:29
  60.9 0.6 collective-permute-start.8
  61.5 3.4 %collective-permute-done.13 = f32[520,256]{1,0:T(8,128)S(1)} collective-permute-done((f32[520,256]{1,0:T(8,128)S(1)}, f32[520,256]{1,0:T(8,128)S(1)}, u32[]{:S(2)}, u32[]{:S(2)}) %collective-permute-start.13) | collective-permute-done | bytes 532512 | tf_op jit(solution)/shard_map/ppermute | solution.py:29
  64.9 6.7 %collective-permute-start.16 = (f32[520,256]{1,0:T(8,128)S(1)}, f32[520,256]{1,0:T(8,128)S(1)}, u32[]{:S(2)}, u32[]{:S(2)}) collective-permute-start(f32[520,256]{1,0:T(8,128)S(1)} %collective-permute-done.13), channel_id=1, source_target_pairs={{0,254},{1,255},{2,0},{3,1},{4,2},{5,3},{6,4},{7,5},{8,6},{9,7},{1... | collective-permute-start | bytes 1597448 | tf_op jit(solution)/shard_map/ppermute | solution.py:29
  71.6 0.3 collective-permute-start.29
  72.0 0.6 collective-permute-start.11
  72.5 7.0 %collective-permute-done.15 = f32[520,256]{1,0:T(8,128)S(1)} collective-permute-done((f32[520,256]{1,0:T(8,128)S(1)}, f32[520,256]{1,0:T(8,128)S(1)}, u32[]{:S(2)}, u32[]{:S(2)}) %collective-permute-start.15) | collective-permute-done | bytes 532512 | tf_op jit(solution)/shard_map/ppermute | solution.py:29
  79.7 0.7 collective-permute-done.16
  80.4 11.8 %collective-permute-done.26 = f32[256,256]{1,0:T(8,128)S(1)} collective-permute-done((f32[256,256]{1,0:T(8,128)S(1)}, f32[256,256]{1,0:T(8,128)S(1)}, u32[]{:S(2)}, u32[]{:S(2)}) %collective-permute-start.26) | collective-permute-done | bytes 262176 | tf_op jit(solution)/shard_map/ppermute | solution.py:29
  92.3 0.3 collective-permute-start.34
  92.6 0.3 collective-permute-start.17
  92.9 1.7 %collective-permute-start.19 = (f32[520,256]{1,0:T(8,128)S(1)}, f32[520,256]{1,0:T(8,128)S(1)}, u32[]{:S(2)}, u32[]{:S(2)}) collective-permute-start(f32[520,256]{1,0:T(8,128)S(1)} %get-tuple-element.108), channel_id=1, source_target_pairs={{0,128},{1,129},{2,130},{3,131},{4,132},{5,133},{6,134},{7,135},{8... | collective-permute-start | bytes 1597448 | tf_op jit(solution)/shard_map/ppermute | solution.py:29
  94.6 0.1 collective-permute-start.28
  94.7 12.5 %collective-permute-done.34.refs_16_ = f32[520,256]{1,0:T(8,128)S(1)} collective-permute-done((f32[520,256]{1,0:T(8,128)S(1)}, f32[520,256]{1,0:T(8,128)S(1)}, u32[]{:S(2)}, u32[]{:S(2)}) %collective-permute-start.34) | collective-permute-done | bytes 532512 | tf_op jit(solution)/shard_map/ppermute | solution.py:29
  107.2 0.5 collective-permute-start.36
  107.8 10.4 %collective-permute-done.19.refs_9_ = f32[520,256]{1,0:T(8,128)S(1)} collective-permute-done((f32[520,256]{1,0:T(8,128)S(1)}, f32[520,256]{1,0:T(8,128)S(1)}, u32[]{:S(2)}, u32[]{:S(2)}) %collective-permute-start.19) | collective-permute-done | bytes 532512 | tf_op jit(solution)/shard_map/ppermute | solution.py:29
  118.2 3.9 %scan.1 = (s32[8]{0:T(128)S(1)}, s32[144]{0:T(256)S(1)}, s32[144]{0:T(256)S(1)}, s32[48]{0:T(128)S(1)}, s32[48]{0:T(128)S(1)}) custom-call(s32[16]{0:T(128)S(1)} %stack.50.info.refs_0_, s32[24]{0:T(128)S(1)} %bitcast.71, s32[24]{0:T(128)S(1)} %bitcast.72, s32[16]{0:T(128)S(1)} %get-tuple-element.121.c_rows.refs_5_, s32[16]{0:T(128)S(1)} %get-tuple-element.120.c_cols.refs_6_, ...), custom_call_target="tpu_custom_call" | custom-call | tf_op jit(solution)/shard_map/scan/pallas_call | solution.py:103
  122.1 0.4 collective-permute-start.18
  122.5 2.1 %multiply.2.refs_16_ = f32[16,256,256]{2,1,0:T(8,128)S(1)} custom-call(s32[16]{0:T(128)S(1)} %stack.50.info.refs_0_, s32[8]{0:T(128)S(1)} %get-tuple-element.95.refs_1_, s32[144]{0:T(256)S(1)} %get-tuple-element.98.refs_2_, s32[144]{0:T(256)S(1)} %get-tuple-element.99.refs_3_, f32[24,256,256]{2,1,0:T(8,128)S(1)} %bitcast.65, f32[6,256,256]{2,1,0:T(8,128)S(1)} %bitcast.70, ...), custom_call_target="tpu_custom_call" | custom-call | flops 268435456 | bytes 12582912 | tf_op jit(solution)/shard_map/multiply/pallas_call | solution.py:244
  124.7 1.1 collective-permute-done.18.refs_4_
  125.8 2.6 %multiply.3 = (f32[8,256,256]{2,1,0:T(8,128)S(1)}, f32[8,256,256]{2,1,0:T(8,128)S(1)}, s32[32]{0:T(128)S(1)}) custom-call(s32[16]{0:T(128)S(1)} %stack.50.info.refs_0_, s32[8]{0:T(128)S(1)} %get-tuple-element.95.refs_1_, s32[48]{0:T(128)S(1)} %get-tuple-element.96.refs_2_, s32[48]{0:T(128)S(1)} %get-tuple-element.97.refs_3_, ...), custom_call_target="tpu_custom_call" | custom-call | flops 268435456 | bytes 12582912 | tf_op jit(solution)/shard_map/multiply/pallas_call | solution.py:244
  128.4 34.2 %conditional.1 = (f32[1,8,256,256]{3,2,1,0:T(8,128)S(1)}) conditional(s32[]{:T(128)} %bitcast.41, (f32[8,256,256]{2,1,0:T(8,128)S(1)}, s32[32]{0:T(128)S(1)}, f32[8,256,256]{2,1,0:T(8,128)S(1)}) %tuple.37, (f32[8,256,256]{2,1,0:T(8,128)S(1)}, s32[32]{0:T(128)S(1)}, f32[8,256,256]{2,1,0:T(8,128)S(1)}) %tuple.37, ...), branch_computations={%region_0.1_spmd, %region_1.2_spmd, %region_2.3_spmd, %region_3.4_... | conditional | bytes 11010096 | solution.py:351
  128.7 0.1 slice.56
  128.8 7.2 %collective-permute-start.4 = (f32[5,256,256]{2,1,0:T(8,128)S(1)}, f32[5,256,256]{2,1,0:T(8,128)S(1)}, u32[]{:S(2)}, u32[]{:S(2)}) collective-permute-start(f32[5,256,256]{2,1,0:T(8,128)S(1)} %slice.56), channel_id=1, source_target_pairs={{0,128},{1,129},{2,130},{3,131},{4,132},{5,133},{6,134},{7,135},{8... | collective-permute-start | bytes 3932168 | tf_op jit(solution)/shard_map/cond/branch_4_fun/ppermute | solution.py:29
  136.0 25.5 %collective-permute-done.4.come = f32[5,256,256]{2,1,0:T(8,128)S(1)} collective-permute-done((f32[5,256,256]{2,1,0:T(8,128)S(1)}, f32[5,256,256]{2,1,0:T(8,128)S(1)}, u32[]{:S(2)}, u32[]{:S(2)}) %collective-permute-start.4) | collective-permute-done | bytes 1310752 | tf_op jit(solution)/shard_map/cond/branch_4_fun/ppermute | solution.py:29
  161.6 1.1 finish.12
  162.6 1.3 copy-done.3
  (67 shorter events, 0.8 us)
Async XLA Ops:
  0.0 37.9 %copy-start.7 = (s32[1,6]{1,0:T(1,128)S(1)}, s32[1,6]{1,0:T(1,128)}, u32[]{:S(2)}) copy-start(s32[1,6]{1,0:T(1,128)} %param.21) | copy-start | bytes 76
  0.0 37.9 %copy-start.6 = (s32[1,6]{1,0:T(1,128)S(1)}, s32[1,6]{1,0:T(1,128)}, u32[]{:S(2)}) copy-start(s32[1,6]{1,0:T(1,128)} %param.22) | copy-start | bytes 76
  0.0 19.1 %copy-start.4 = (s32[1,16]{1,0:T(1,128)S(1)}, s32[1,16]{1,0:T(1,128)}, u32[]{:S(2)}) copy-start(s32[1,16]{1,0:T(1,128)} %param.25) | copy-start | bytes 196
  0.0 19.2 %copy-start.5 = (s32[1,16]{1,0:T(1,128)S(1)}, s32[1,16]{1,0:T(1,128)}, u32[]{:S(2)}) copy-start(s32[1,16]{1,0:T(1,128)} %param.24) | copy-start | bytes 196
  0.7 121.8 %slice-start = ((s8[6291456]{0:T(1024)(128)(4,1)}), s8[2097152]{0:T(1024)(128)(4,1)S(1)}, s32[]{:S(2)}) async-start(s8[6291456]{0:T(1024)(128)(4,1)} %bitcast.63), calls=%async_computation | async-start | bytes 4194304
  3.6 34.6 %collective-permute-start.9 = (f32[520,256]{1,0:T(8,128)}, f32[520,256]{1,0:T(8,128)S(1)}, u32[]{:S(2)}, u32[]{:S(2)}) collective-permute-start(f32[520,256]{1,0:T(8,128)} %select_maximum_fusion), channel_id=1, source_target_pairs={{0,2},{1,3},{2,4},{3,5},{4,6},{5,7},{6,8},{7,9},{8,10},{9,11},{10,... | collective-permute-start | bytes 1597448 | tf_op jit(solution)/shard_map/ppermute | solution.py:29
  5.5 43.9 %collective-permute-start.10 = (f32[520,256]{1,0:T(8,128)}, f32[520,256]{1,0:T(8,128)S(1)}, u32[]{:S(2)}, u32[]{:S(2)}) collective-permute-start(f32[520,256]{1,0:T(8,128)} %select_maximum_fusion), channel_id=1, source_target_pairs={{0,254},{1,255},{2,0},{3,1},{4,2},{5,3},{6,4},{7,5},{8,6},{9,7},{1... | collective-permute-start | bytes 1597448 | tf_op jit(solution)/shard_map/ppermute | solution.py:29
  12.8 17.1 %collective-permute-start.20 = (f32[256,256]{1,0:T(8,128)S(1)}, f32[256,256]{1,0:T(8,128)}, u32[]{:S(2)}, u32[]{:S(2)}) collective-permute-start(f32[256,256]{1,0:T(8,128)S(1)} %dynamic-slice_bitcast_fusion), channel_id=1, source_target_pairs={{0,2},{1,3},{2,4},{3,5},{4,6},{5,7},{6,8},{7,9},{8,10},{9,11},{10,... | collective-permute-start | bytes 786440 | tf_op jit(solution)/shard_map/ppermute | solution.py:29
  12.9 17.0 %collective-permute-start.23 = (f32[256,256]{1,0:T(8,128)S(1)}, f32[256,256]{1,0:T(8,128)}, u32[]{:S(2)}, u32[]{:S(2)}) collective-permute-start(f32[256,256]{1,0:T(8,128)S(1)} %dynamic-slice_bitcast_fusion), channel_id=1, source_target_pairs={{0,254},{1,255},{2,0},{3,1},{4,2},{5,3},{6,4},{7,5},{8,6},{9,7},{1... | collective-permute-start | bytes 786440 | tf_op jit(solution)/shard_map/ppermute | solution.py:29
  29.9 12.0 %collective-permute-start.21 = (f32[256,256]{1,0:T(8,128)}, f32[256,256]{1,0:T(8,128)}, u32[]{:S(2)}, u32[]{:S(2)}) collective-permute-start(f32[256,256]{1,0:T(8,128)} %collective-permute-done.20), channel_id=1, source_target_pairs={{0,2},{1,3},{2,4},{3,5},{4,6},{5,7},{6,8},{7,9},{8,10},{9,11},{10,... | collective-permute-start | bytes 786440 | tf_op jit(solution)/shard_map/ppermute | solution.py:29
  29.9 12.0 %collective-permute-start.24 = (f32[256,256]{1,0:T(8,128)}, f32[256,256]{1,0:T(8,128)}, u32[]{:S(2)}, u32[]{:S(2)}) collective-permute-start(f32[256,256]{1,0:T(8,128)} %collective-permute-done.23), channel_id=1, source_target_pairs={{0,254},{1,255},{2,0},{3,1},{4,2},{5,3},{6,4},{7,5},{8,6},{9,7},{1... | collective-permute-start | bytes 786440 | tf_op jit(solution)/shard_map/ppermute | solution.py:29
  37.9 8.2 %collective-permute-start.31 = (f32[256,256]{1,0:T(8,128)}, f32[256,256]{1,0:T(8,128)}, u32[]{:S(2)}, u32[]{:S(2)}) collective-permute-start(f32[256,256]{1,0:T(8,128)} %get-tuple-element.113), channel_id=1, source_target_pairs={{0,128},{1,129},{2,130},{3,131},{4,132},{5,133},{6,134},{7,135},{8... | collective-permute-start | bytes 786440 | tf_op jit(solution)/shard_map/ppermute | solution.py:29
  38.2 22.6 %collective-permute-start.12 = (f32[520,256]{1,0:T(8,128)S(1)}, f32[520,256]{1,0:T(8,128)S(1)}, u32[]{:S(2)}, u32[]{:S(2)}) collective-permute-start(f32[520,256]{1,0:T(8,128)S(1)} %collective-permute-done.9), channel_id=1, source_target_pairs={{0,2},{1,3},{2,4},{3,5},{4,6},{5,7},{6,8},{7,9},{8,10},{9,11},{10,... | collective-permute-start | bytes 1597448 | tf_op jit(solution)/shard_map/ppermute | solution.py:29
  43.0 28.6 %collective-permute-start.35 = (f32[256,256]{1,0:T(8,128)S(1)}, f32[256,256]{1,0:T(8,128)S(1)}, u32[]{:S(2)}, u32[]{:S(2)}) collective-permute-start(f32[256,256]{1,0:T(8,128)S(1)} %get-tuple-element.111), channel_id=1, source_target_pairs={{0,128},{1,129},{2,130},{3,131},{4,132},{5,133},{6,134},{7,135},{8... | collective-permute-start | bytes 786440 | tf_op jit(solution)/shard_map/ppermute | solution.py:29
  43.1 17.8 %collective-permute-start.22 = (f32[256,256]{1,0:T(8,128)}, f32[256,256]{1,0:T(8,128)S(1)}, u32[]{:S(2)}, u32[]{:S(2)}) collective-permute-start(f32[256,256]{1,0:T(8,128)} %collective-permute-done.21), channel_id=1, source_target_pairs={{0,2},{1,3},{2,4},{3,5},{4,6},{5,7},{6,8},{7,9},{8,10},{9,11},{10,... | collective-permute-start | bytes 786440 | tf_op jit(solution)/shard_map/ppermute | solution.py:29
  46.1 14.7 %collective-permute-start.25 = (f32[256,256]{1,0:T(8,128)}, f32[256,256]{1,0:T(8,128)S(1)}, u32[]{:S(2)}, u32[]{:S(2)}) collective-permute-start(f32[256,256]{1,0:T(8,128)} %collective-permute-done.24), channel_id=1, source_target_pairs={{0,254},{1,255},{2,0},{3,1},{4,2},{5,3},{6,4},{7,5},{8,6},{9,7},{1... | collective-permute-start | bytes 786440 | tf_op jit(solution)/shard_map/ppermute | solution.py:29
  49.4 15.5 %collective-permute-start.13 = (f32[520,256]{1,0:T(8,128)S(1)}, f32[520,256]{1,0:T(8,128)S(1)}, u32[]{:S(2)}, u32[]{:S(2)}) collective-permute-start(f32[520,256]{1,0:T(8,128)S(1)} %collective-permute-done.10), channel_id=1, source_target_pairs={{0,254},{1,255},{2,0},{3,1},{4,2},{5,3},{6,4},{7,5},{8,6},{9,7},{1... | collective-permute-start | bytes 1597448 | tf_op jit(solution)/shard_map/ppermute | solution.py:29
  51.1 20.5 %copy-start = (f32[1,6,256,256]{3,2,1,0:T(8,128)S(1)}, f32[1,6,256,256]{3,2,1,0:T(8,128)}, u32[]{:S(2)}) copy-start(f32[1,6,256,256]{3,2,1,0:T(8,128)} %param.20) | copy-start | bytes 4718596
  52.2 70.3 %slice-start.1 = ((s8[6291456]{0:T(1024)(128)(4,1)}), s8[4194304]{0:T(1024)(128)(4,1)S(1)}, s32[]{:S(2)}) async-start(s8[6291456]{0:T(1024)(128)(4,1)} %bitcast.63), calls=%async_computation.1 | async-start | bytes 8388608
  60.8 11.7 %collective-permute-start.33 = (f32[512,256]{1,0:T(8,128)S(1)}, f32[512,256]{1,0:T(8,128)S(1)}, u32[]{:S(2)}, u32[]{:S(2)}) collective-permute-start(f32[512,256]{1,0:T(8,128)S(1)} %pad_maximum_fusion.1.refs_9_.refs_10_), channel_id=1, source_target_pairs={{0,1},{1,0},{2,3},{3,2},{4,5},{5,4},{6,7},{7,6},{8,9},{9,8},{10,11... | collective-permute-start | bytes 1572872 | tf_op jit(solution)/shard_map/ppermute | solution.py:29
  60.8 18.7 %collective-permute-start.15 = (f32[520,256]{1,0:T(8,128)S(1)}, f32[520,256]{1,0:T(8,128)S(1)}, u32[]{:S(2)}, u32[]{:S(2)}) collective-permute-start(f32[520,256]{1,0:T(8,128)S(1)} %collective-permute-done.12), channel_id=1, source_target_pairs={{0,2},{1,3},{2,4},{3,5},{4,6},{5,7},{6,8},{7,9},{8,10},{9,11},{10,... | collective-permute-start | bytes 1597448 | tf_op jit(solution)/shard_map/ppermute | solution.py:29
  60.9 11.1 %collective-permute-start.8 = (s32[16]{0:T(128)S(1)}, s32[16]{0:T(128)S(1)}, u32[]{:S(2)}, u32[]{:S(2)}) collective-permute-start(s32[16]{0:T(128)S(1)} %pad_add_fusion.refs_0_), channel_id=1, source_target_pairs={{0,1},{1,0},{2,3},{3,2},{4,5},{5,4},{6,7},{7,6},{8,9},{9,8},{10,11... | collective-permute-start | bytes 200 | tf_op jit(solution)/shard_map/ppermute | solution.py:29
  64.9 15.5 %collective-permute-start.16 = (f32[520,256]{1,0:T(8,128)S(1)}, f32[520,256]{1,0:T(8,128)S(1)}, u32[]{:S(2)}, u32[]{:S(2)}) collective-permute-start(f32[520,256]{1,0:T(8,128)S(1)} %collective-permute-done.13), channel_id=1, source_target_pairs={{0,254},{1,255},{2,0},{3,1},{4,2},{5,3},{6,4},{7,5},{8,6},{9,7},{1... | collective-permute-start | bytes 1597448 | tf_op jit(solution)/shard_map/ppermute | solution.py:29
  71.6 50.5 %collective-permute-start.29 = (f32[6,256,256]{2,1,0:T(8,128)S(1)}, f32[6,256,256]{2,1,0:T(8,128)S(1)}, u32[]{:S(2)}, u32[]{:S(2)}) collective-permute-start(f32[6,256,256]{2,1,0:T(8,128)S(1)} %bitcast.69), channel_id=1, source_target_pairs={{0,1},{1,0},{2,3},{3,2},{4,5},{5,4},{6,7},{7,6},{8,9},{9,8},{10,11... | collective-permute-start | bytes 4718600 | tf_op jit(solution)/shard_map/ppermute | solution.py:29
  72.0 20.3 %collective-permute-start.11 = (f32[520,256]{1,0:T(8,128)S(1)}, f32[520,256]{1,0:T(8,128)S(1)}, u32[]{:S(2)}, u32[]{:S(2)}) collective-permute-start(f32[520,256]{1,0:T(8,128)S(1)} %get-tuple-element.107.refs_7_), channel_id=1, source_target_pairs={{0,1},{1,0},{2,3},{3,2},{4,5},{5,4},{6,7},{7,6},{8,9},{9,8},{10,11... | collective-permute-start | bytes 1597448 | tf_op jit(solution)/shard_map/ppermute | solution.py:29
  72.5 20.0 %collective-permute-start.30 = (f32[520,256]{1,0:T(8,128)S(1)}, f32[520,256]{1,0:T(8,128)S(1)}, u32[]{:S(2)}, u32[]{:S(2)}) collective-permute-start(f32[520,256]{1,0:T(8,128)S(1)} %get-tuple-element.106), channel_id=1, source_target_pairs={{0,128},{1,129},{2,130},{3,131},{4,132},{5,133},{6,134},{7,135},{8... | collective-permute-start | bytes 1597448 | tf_op jit(solution)/shard_map/ppermute | solution.py:29
  79.6 13.3 %collective-permute-start.37 = (f32[512,256]{1,0:T(8,128)S(1)}, f32[512,256]{1,0:T(8,128)S(1)}, u32[]{:S(2)}, u32[]{:S(2)}) collective-permute-start(f32[512,256]{1,0:T(8,128)S(1)} %pad_maximum_fusion.2.refs_17_.refs_18_), channel_id=1, source_target_pairs={{0,1},{1,0},{2,3},{3,2},{4,5},{5,4},{6,7},{7,6},{8,9},{9,8},{10,11... | collective-permute-start | bytes 1572872 | tf_op jit(solution)/shard_map/ppermute | solution.py:29
  79.6 38.6 %copy-start.1 = (s32[1,24]{1,0:T(1,128)S(1)}, s32[1,24]{1,0:T(1,128)}, u32[]{:S(2)}) copy-start(s32[1,24]{1,0:T(1,128)} %param.18) | copy-start | bytes 292
  79.7 38.6 %copy-start.2 = (s32[1,24]{1,0:T(1,128)S(1)}, s32[1,24]{1,0:T(1,128)}, u32[]{:S(2)}) copy-start(s32[1,24]{1,0:T(1,128)} %param.19) | copy-start | bytes 292
  80.3 11.9 %collective-permute-start.26 = (f32[256,256]{1,0:T(8,128)S(1)}, f32[256,256]{1,0:T(8,128)S(1)}, u32[]{:S(2)}, u32[]{:S(2)}) collective-permute-start(f32[256,256]{1,0:T(8,128)S(1)} %get-tuple-element.115), channel_id=1, source_target_pairs={{0,128},{1,129},{2,130},{3,131},{4,132},{5,133},{6,134},{7,135},{8... | collective-permute-start | bytes 786440 | tf_op jit(solution)/shard_map/ppermute | solution.py:29
  92.3 2.3 %collective-permute-start.14 = (f32[520,256]{1,0:T(8,128)S(1)}, f32[520,256]{1,0:T(8,128)S(1)}, u32[]{:S(2)}, u32[]{:S(2)}) collective-permute-start(f32[520,256]{1,0:T(8,128)S(1)} %get-tuple-element.105.refs_15_), channel_id=1, source_target_pairs={{0,1},{1,0},{2,3},{3,2},{4,5},{5,4},{6,7},{7,6},{8,9},{9,8},{10,11... | collective-permute-start | bytes 1597448 | tf_op jit(solution)/shard_map/ppermute | solution.py:29
  92.3 15.0 %collective-permute-start.34 = (f32[520,256]{1,0:T(8,128)S(1)}, f32[520,256]{1,0:T(8,128)S(1)}, u32[]{:S(2)}, u32[]{:S(2)}) collective-permute-start(f32[520,256]{1,0:T(8,128)S(1)} %get-tuple-element.104), channel_id=1, source_target_pairs={{0,128},{1,129},{2,130},{3,131},{4,132},{5,133},{6,134},{7,135},{8... | collective-permute-start | bytes 1597448 | tf_op jit(solution)/shard_map/ppermute | solution.py:29
  92.6 14.7 %collective-permute-start.17 = (f32[520,256]{1,0:T(8,128)S(1)}, f32[520,256]{1,0:T(8,128)S(1)}, u32[]{:S(2)}, u32[]{:S(2)}) collective-permute-start(f32[520,256]{1,0:T(8,128)S(1)} %get-tuple-element.109.refs_8_), channel_id=1, source_target_pairs={{0,1},{1,0},{2,3},{3,2},{4,5},{5,4},{6,7},{7,6},{8,9},{9,8},{10,11... | collective-permute-start | bytes 1597448 | tf_op jit(solution)/shard_map/ppermute | solution.py:29
  92.9 25.3 %collective-permute-start.19 = (f32[520,256]{1,0:T(8,128)S(1)}, f32[520,256]{1,0:T(8,128)S(1)}, u32[]{:S(2)}, u32[]{:S(2)}) collective-permute-start(f32[520,256]{1,0:T(8,128)S(1)} %get-tuple-element.108), channel_id=1, source_target_pairs={{0,128},{1,129},{2,130},{3,131},{4,132},{5,133},{6,134},{7,135},{8... | collective-permute-start | bytes 1597448 | tf_op jit(solution)/shard_map/ppermute | solution.py:29
  94.6 30.1 %collective-permute-start.28 = (f32[512,256]{1,0:T(8,128)S(1)}, f32[512,256]{1,0:T(8,128)S(1)}, u32[]{:S(2)}, u32[]{:S(2)}) collective-permute-start(f32[512,256]{1,0:T(8,128)S(1)} %pad_maximum_fusion.refs_10_.refs_11_), channel_id=1, source_target_pairs={{0,1},{1,0},{2,3},{3,2},{4,5},{5,4},{6,7},{7,6},{8,9},{9,8},{10,11... | collective-permute-start | bytes 1572872 | tf_op jit(solution)/shard_map/ppermute | solution.py:29
  107.2 15.3 %collective-permute-start.32 = (f32[520,256]{1,0:T(8,128)S(1)}, f32[520,256]{1,0:T(8,128)S(1)}, u32[]{:S(2)}, u32[]{:S(2)}) collective-permute-start(f32[520,256]{1,0:T(8,128)S(1)} %collective-permute-done.30.refs_8_), channel_id=1, source_target_pairs={{0,1},{1,0},{2,3},{3,2},{4,5},{5,4},{6,7},{7,6},{8,9},{9,8},{10,11... | collective-permute-start | bytes 1597448 | tf_op jit(solution)/shard_map/ppermute | solution.py:29
  107.2 15.3 %collective-permute-start.36 = (f32[520,256]{1,0:T(8,128)S(1)}, f32[520,256]{1,0:T(8,128)S(1)}, u32[]{:S(2)}, u32[]{:S(2)}) collective-permute-start(f32[520,256]{1,0:T(8,128)S(1)} %collective-permute-done.34.refs_16_), channel_id=1, source_target_pairs={{0,1},{1,0},{2,3},{3,2},{4,5},{5,4},{6,7},{7,6},{8,9},{9,8},{10,11... | collective-permute-start | bytes 1597448 | tf_op jit(solution)/shard_map/ppermute | solution.py:29
  118.2 7.6 %collective-permute-start.27 = (f32[520,256]{1,0:T(8,128)S(1)}, f32[520,256]{1,0:T(8,128)S(1)}, u32[]{:S(2)}, u32[]{:S(2)}) collective-permute-start(f32[520,256]{1,0:T(8,128)S(1)} %collective-permute-done.19.refs_9_), channel_id=1, source_target_pairs={{0,1},{1,0},{2,3},{3,2},{4,5},{5,4},{6,7},{7,6},{8,9},{9,8},{10,11... | collective-permute-start | bytes 1597448 | tf_op jit(solution)/shard_map/ppermute | solution.py:29
  122.1 3.7 %collective-permute-start.18 = (s32[8]{0:T(128)S(1)}, s32[8]{0:T(128)S(1)}, u32[]{:S(2)}, u32[]{:S(2)}) collective-permute-start(s32[8]{0:T(128)S(1)} %get-tuple-element.95.refs_1_), channel_id=1, source_target_pairs={{0,128},{1,129},{2,130},{3,131},{4,132},{5,133},{6,134},{7,135},{8... | collective-permute-start | bytes 104 | tf_op jit(solution)/shard_map/ppermute | solution.py:29
  128.8 32.8 %collective-permute-start.4 = (f32[5,256,256]{2,1,0:T(8,128)S(1)}, f32[5,256,256]{2,1,0:T(8,128)S(1)}, u32[]{:S(2)}, u32[]{:S(2)}) collective-permute-start(f32[5,256,256]{2,1,0:T(8,128)S(1)} %slice.56), channel_id=1, source_target_pairs={{0,128},{1,129},{2,130},{3,131},{4,132},{5,133},{6,134},{7,135},{8... | collective-permute-start | bytes 3932168 | tf_op jit(solution)/shard_map/cond/branch_4_fun/ppermute | solution.py:29
  162.6 1.3 copy-start.3
